TPU v7x, 256 devices: a whole 4x4x8 slice. The times are simulated.
256 devices in a mesh: frame: 8 (over z), tile: 32 (over x, y, core).
Axes of the slice: x: 4, y: 4, z: 8, core: 2. Of those that a mesh axis runs over, the one named last changes fastest.
Arguments:
- displacement: bfloat16 [512, 2, 32, 4096], P('frame', None, 'tile'), may hold values from -256 to 256
Outputs:
- basis: bfloat16 [512, 3, 32, 4096], P(None, None, 'tile', 'frame')
- factor: float32 [512, 512], replicated
All inputs are finite; a program needn't handle non-finite values.
Results may differ from a plain program's by a relative error of at most 0.0053.
The roundings to bfloat16 on the way count: a program that leaves them out, or rounds other values in their place, can miss the bound.
Values may be sent and summed in bfloat16 or wider, within the bound.
No kernel may reach another device: no remote copies, remote signals or barrier semaphores. Data moves between devices by JAX's collectives and lax.ppermute only.
A program may use at most 64 MiB of HBM per device.

v0:
```python
import math

import jax
import jax.numpy as jnp
from jax import lax
from jax.sharding import PartitionSpec as P


def with_halo(array, sides, width):
    for axis, dim in sides:
        peers, length = (lax.axis_size(axis), array.shape[dim])
        up = [(i, (i + 1) % peers) for i in range(peers - 1)]
        down = [(j, i) for i, j in up]
        last = lax.slice_in_dim(array, length - width, length, axis=dim)
        first = lax.slice_in_dim(array, 0, width, axis=dim)
        before = lax.ppermute(last, axis, up)
        after = lax.ppermute(first, axis, down)
        array = jnp.concatenate([before, array, after], axis=dim)
    return array


def derivative(center, before, after, first, final):
    return jnp.where(
        first, after - center, jnp.where(final, center - before, (after - before) * 0.5)
    )


def column_derivative(center):
    width = center.shape[-1]
    after = jnp.concatenate([center[..., 1:], center[..., -1:]], axis=-1)
    before = jnp.concatenate([center[..., :1], center[..., :-1]], axis=-1)
    column = jnp.arange(width, dtype=jnp.int32)
    return derivative(center, before, after, column == 0, column == width - 1)


def combine_strain(d_rows, d_cols):
    return jnp.stack(
        [d_cols[:, 0], d_rows[:, 1], 0.5 * (d_rows[:, 0] + d_cols[:, 1])], axis=1
    ).astype(jnp.bfloat16)


def local(displacement):
    rows = displacement.shape[2]
    full_width = displacement.shape[3]
    total_rows = lax.axis_size("tile") * rows
    scale = math.sqrt(3 * total_rows * full_width)
    row_global = lax.axis_index("tile") * rows + jnp.arange(rows, dtype=jnp.int32)
    first = (row_global == 0)[:, None]
    final = (row_global == total_rows - 1)[:, None]
    padded = with_halo(displacement, (("tile", 2),), 1)
    field = padded.astype(jnp.float32)
    center = field[:, :, 1:-1, :]
    d_rows = derivative(center, field[:, :, :-2, :], field[:, :, 2:, :], first, final)
    d_cols = column_derivative(center)
    strain = combine_strain(d_rows, d_cols)
    pixel_major = lax.all_to_all(strain, "frame", split_axis=3, concat_axis=0, tiled=True)
    frames = pixel_major.shape[0]
    snapshot_half = pixel_major.reshape(frames, -1)
    local_gram = lax.dot_general(
        snapshot_half, snapshot_half, (((1,), (1,)), ((), ())), preferred_element_type=jnp.float32
    )
    gram = lax.psum(local_gram, ("frame", "tile"))
    lower = jnp.linalg.cholesky(gram)
    snapshot = snapshot_half.astype(jnp.float32)
    solved = lax.linalg.triangular_solve(lower, snapshot, left_side=True, lower=True)
    basis = (solved * scale).astype(jnp.bfloat16).reshape(pixel_major.shape)
    return (basis, lower.T / scale)


def solution(mesh):
    return jax.shard_map(
        local,
        mesh=mesh,
        in_specs=(P("frame", None, "tile", None),),
        out_specs=(P(None, None, "tile", "frame"), P()),
        check_vma=False,
    )
```

profile of v0, /device:TPU:1, one launch (start us, length us, event | category | flops | bytes accessed | tf_op | source)
XLA Modules:
  0.0 526.2 jit_solution(18431249091505621572)
XLA Ops:
  7.2 1.8 copy.46
  9.0 4.6 collective-permute-start
  13.6 1.9 collective-permute-start.1
  15.6 9.8 %collective-permute-done = bf16[64,2,1,4096]{3,0,2,1:T(8,128)(2,1)S(1)} collective-permute-done((bf16[64,2,1,4096]{3,0,2,1:T(8,128)(2,1)S(1)}, bf16[64,2,1,4096]{3,0,2,1:T(8,128)(2,1)S(1)}, u32[]{:S(2)}, u32[]{:S(2)}) %collective-permute-start) | collective-permute-done | bytes 1048608 | tf_op jit(solution)/shard_map/ppermute | solution.py:16
  25.3 4.4 collective-permute-done.1
  29.7 0.5 maximum_convert_fusion
  30.2 0.7 fusion.35
  31.0 1.5 select_select_fusion
  32.9 4.7 copy.49
  37.7 6.1 %reshape.243 = bf16[8,2,49152]{2,1,0:T(2,128)(2,1)S(1)} reshape(bf16[4096,1,3,64]{3,2,1,0:T(4,128)(2,1)} %bitcast.77) | data formatting | bytes 3145728
  43.8 37.4 %all_to_all.15 = bf16[8,2,49152]{2,1,0:T(2,128)(2,1)S(1)} all-to-all(bf16[8,2,49152]{2,1,0:T(2,128)(2,1)S(1)} %reshape.243), channel_id=1, replica_groups=mesh['frame'=8,'tile'=32] {'frame'}, dimensions={0} | all-to-all | bytes 3145728 | tf_op jit(solution)/shard_map/all_to_all | solution.py:56
  81.2 4.8 reshape.244
  86.0 4.5 copy.67
  90.5 1.4 copy.51
  91.9 0.5 copy.69
  92.4 2.0 fusion.36
  94.6 2.1 convert_element_type.26
  96.7 0.3 copy.54
  97.1 0.8 copy.70
  97.9 257.6 %all-reduce.3.cloned.1.call-done = f32[512,512]{0,1:T(8,128)} async-done(((f32[512,512]{0,1:T(8,128)}), f32[512,512]{0,1:T(8,128)}) %all-reduce.3.cloned.1.call-update) | async-done | bytes 1048592 | tf_op jit(solution)/shard_map/psum | solution.py:62
  355.5 1.6 copy.53
  357.5 11.7 %cholesky.104 = f32[128,128]{1,0:T(8,128)S(1)} custom-call(f32[128,128]{1,0:T(8,128)S(1)} %cholesky.266), custom_call_target="Cholesky" | custom-call | tf_op jit(solution)/shard_map/jit(cholesky)/cholesky | solution.py:63
  369.3 9.8 %custom-call.30 = f32[1,128,128]{1,2,0:T(8,128)S(1)} custom-call(f32[1,128,128]{2,1,0:T(8,128)S(1)} %get-tuple-element.45), custom_call_target="InvertDiagBlocksLowerTriangular" | custom-call | tf_op jit(solution)/shard_map/jit(cholesky)/cholesky | solution.py:63
  379.1 0.3 constant_dynamic-update-slice_fusion.3
  379.5 0.3 convolution_subtract_fusion.3
  379.8 12.1 %cholesky.217 = f32[128,128]{1,0:T(8,128)S(1)} custom-call(f32[128,128]{1,0:T(8,128)S(1)} %cholesky.270), custom_call_target="Cholesky" | custom-call | tf_op jit(solution)/shard_map/jit(cholesky)/cholesky | solution.py:63
  391.9 0.6 compare_reduce_fusion.2
  392.5 0.6 compare_reduce_fusion.3
  393.2 9.8 %custom-call.31 = f32[1,128,128]{1,2,0:T(8,128)S(1)} custom-call(f32[1,128,128]{2,1,0:T(8,128)S(1)} %get-tuple-element.42), custom_call_target="InvertDiagBlocksLowerTriangular" | custom-call | tf_op jit(solution)/shard_map/jit(cholesky)/cholesky | solution.py:63
  403.0 0.3 convolution_dynamic-update-slice_fusion
  403.3 0.4 convolution_subtract_fusion.4
  403.7 11.7 %cholesky.238 = f32[128,128]{1,0:T(8,128)S(1)} custom-call(f32[128,128]{1,0:T(8,128)S(1)} %cholesky.275), custom_call_target="Cholesky" | custom-call | tf_op jit(solution)/shard_map/jit(cholesky)/cholesky | solution.py:63
  415.4 0.7 compare_reduce_fusion.1
  416.1 9.8 %custom-call.32 = f32[1,128,128]{1,2,0:T(8,128)S(1)} custom-call(f32[1,128,128]{2,1,0:T(8,128)S(1)} %get-tuple-element.39), custom_call_target="InvertDiagBlocksLowerTriangular" | custom-call | tf_op jit(solution)/shard_map/jit(cholesky)/cholesky | solution.py:63
  426.1 0.4 convolution_subtract_fusion.5
  426.5 11.9 %cholesky.255 = f32[128,128]{1,0:T(8,128)S(1)} custom-call(f32[128,128]{1,0:T(8,128)S(1)} %convolution_subtract_fusion.5), custom_call_target="Cholesky" | custom-call | tf_op jit(solution)/shard_map/jit(cholesky)/cholesky | solution.py:63
  438.4 0.7 compare_reduce_fusion
  441.6 0.3 multiply_bitcast_fusion
  441.9 10.0 %while.1 = (s32[]{:T(128)}, f32[512,512]{1,0:T(8,128)S(1)}, s32[4,2]{0,1:T(2,128)S(1)}, f32[4,128,128]{2,1,0:T(8,128)}, s32[]{:T(128)}) while((s32[]{:T(128)}, f32[512,512]{1,0:T(8,128)S(1)}, s32[4,2]{0,1:T(2,128)S(1)}, f32[4,128,128]{2,1,0:T(8,128)}, s32[]{:T(128)}) %tuple.39), condition=%wide.while_cond, body=%wide.while_body.sunk | while | flops 2 | bytes 132705 | solution.py:65
  442.0 0.5 fusion.46
  442.5 1.9 bitcast_dynamic-update-slice_fusion.2
  444.5 0.5 fusion.46
  445.0 1.9 bitcast_dynamic-update-slice_fusion.2
  447.0 0.5 fusion.46
  447.5 1.9 bitcast_dynamic-update-slice_fusion.2
  449.5 0.5 fusion.46
  450.0 1.9 bitcast_dynamic-update-slice_fusion.2
  451.9 40.2 %custom-call.33 = f32[4,128,128]{1,2,0:T(8,128)S(1)} custom-call(f32[4,128,128]{2,1,0:T(8,128)} %get-tuple-element.9), custom_call_target="InvertDiagBlocksLowerTriangular" | custom-call | tf_op jit(solution)/shard_map/triangular_solve | solution.py:65
  492.1 1.6 fusion.26
  493.7 2.1 convolution_subtract_fusion.2
  495.8 1.7 fusion.25
  497.6 1.9 convolution_subtract_fusion
  499.5 1.7 fusion.23
  501.2 3.4 fusion.1
  504.6 1.1 copy.57
  505.7 1.2 copy.56
  506.9 1.1 copy.55
  508.0 1.4 copy.58
  509.4 1.7 convolution_bitcast_fusion
  511.1 0.3 copy.62
  511.4 1.4 copy.61
  512.8 2.3 copy.60
  515.1 1.3 copy.64
  516.4 2.7 fusion.7
  (36 shorter events, 1.8 us)
Async XLA Ops:
  7.2 348.4 %all-reduce.3.cloned.1.call-start = ((), (), s32[]{:S(2)}) async-start(), calls=%async_computation.1 | async-start | bytes 2097152 | tf_op jit(solution)/shard_map/psum | solution.py:62
  9.0 16.3 %collective-permute-start = (bf16[64,2,1,4096]{3,0,2,1:T(8,128)(2,1)S(1)}, bf16[64,2,1,4096]{3,0,2,1:T(8,128)(2,1)S(1)}, u32[]{:S(2)}, u32[]{:S(2)}) collective-permute-start(bf16[64,2,1,4096]{3,0,2,1:T(8,128)(2,1)S(1)} %copy.46), channel_id=1, source_target_pairs={{0,1},{1,2},{2,3},{3,4},{4,5},{5,6},{6,7},{7,8},{8,9},{9,10},{10,1... | collective-permute-start | bytes 3145736 | tf_op jit(solution)/shard_map/ppermute | solution.py:16
  13.6 16.1 %collective-permute-start.1 = (bf16[64,2,1,4096]{3,0,2,1:T(8,128)(2,1)S(1)}, bf16[64,2,1,4096]{3,0,2,1:T(8,128)(2,1)S(1)}, u32[]{:S(2)}, u32[]{:S(2)}) collective-permute-start(bf16[64,2,1,4096]{3,0,2,1:T(8,128)(2,1)S(1)} %copy.46), channel_id=1, source_target_pairs={{1,0},{2,1},{3,2},{4,3},{5,4},{6,5},{7,6},{8,7},{9,8},{10,9},{11,1... | collective-permute-start | bytes 3145736 | tf_op jit(solution)/shard_map/ppermute | solution.py:17
  355.5 1.7 copy-start.1
  451.9 40.2 %copy-start.3 = (f32[512,512]{1,0:T(8,128)}, f32[512,512]{1,0:T(8,128)S(1)}, u32[]{:S(2)}) copy-start(f32[512,512]{1,0:T(8,128)S(1)} %get-tuple-element.100) | copy-start | bytes 3145732
  492.1 1.6 copy-start.4
  493.7 3.8 copy-start
  506.9 4.3 copy-start.2
Sparse Core Ops, SparseCore 0:
  94.5 260.9 all-reduce.2
where the time goes:
time: 532 us; the launch traced here: 526 us
  waiting for transfers between devices  272 us (51%)
  other arithmetic  127 us (24%)
  local copies, waits for them, and re-layouts  48 us (9%)
  blocking collectives  37.4 us (7%)
  matrix products  17.9 us (3%)
  between operations  17.1 us (3%)
  starting transfers between devices  6.55 us (1%)
    psum x1, waiting for transfers between devices, local(): gram = lax.psum(local_gram, ('frame', 'tile'))  258 us
    another operation x15, other arithmetic, local(): lower = jnp.linalg.cholesky(gram)  79.6 us
    another operation x2, other arithmetic, local(): lax.linalg.triangular_solve(lower, snapshot, left_side=True, lower=True)  40.2 us
    all_to_all x1, blocking collectives, local(): lax.all_to_all(strain, 'frame', split_axis=3, concat_axis=0, tiled=True)  37.4 us
    unnamed x16, local copies, waits for them, and re-layouts  15.4 us
    another operation x7, matrix products, local(): lax.linalg.triangular_solve(lower, snapshot, left_side=True, lower=True)  14.1 us
  transfers between devices with their start and end apart: 3, of which 3 were waited for; matrix products, arithmetic and copies ran while one was open for 1% of the time, Pallas kernels for 0%

commit v1 on v0

v1 whole, which is shorter than its diff:
```python
import functools
import math

import jax
import jax.numpy as jnp
from jax import lax
from jax.experimental import pallas as pl
from jax.experimental.pallas import tpu as pltpu
from jax.sharding import Mesh, PartitionSpec as P

TILE = ("x", "y", "core")
SUB = 8
BLOCK = 128
HIGH = lax.Precision.HIGHEST
F32 = jnp.float32
BF16 = jnp.bfloat16
VMEM = pl.BlockSpec(memory_space=pltpu.VMEM)
SMEM = pl.BlockSpec(memory_space=pltpu.SMEM)
PARAMS = pltpu.CompilerParams(vmem_limit_bytes=40 << 20)


def column_derivative(center):
    width = center.shape[-1]
    column = lax.broadcasted_iota(jnp.int32, center.shape, center.ndim - 1)
    first, final = column == 0, column == width - 1
    after = jnp.where(final, center, pltpu.roll(center, width - 1, center.ndim - 1))
    before = jnp.where(first, center, pltpu.roll(center, 1, center.ndim - 1))
    return (after - before) * jnp.where(first | final, 1.0, 0.5)


def row_derivative(center, before, after, first, final):
    after = jnp.where(final, center, after)
    before = jnp.where(first, center, before)
    return (after - before) * jnp.where(first | final, 1.0, 0.5)


def scatter_columns(whole_ref, place, outs):
    peers = len(outs)
    width = outs[0].shape[-1]
    for shift in range(peers):
        start = pl.multiple_of(lax.rem(place + shift, peers) * width, width)
        outs[shift][...] = whole_ref[..., pl.ds(start, width)]


def normal_kernel(where_ref, center_ref, *refs):
    outs, whole_ref = refs[:-1], refs[-1]
    whole_ref[...] = column_derivative(center_ref[0].astype(F32)).astype(BF16)
    scatter_columns(whole_ref, where_ref[0], outs)


def shear_kernel(where_ref, center_ref, before_ref, after_ref, *refs):
    outs, whole_ref = refs[:-1], refs[-1]
    first, final = where_ref[1] == 0, where_ref[1] == where_ref[2] - 1
    u, v = center_ref[0].astype(F32), center_ref[1].astype(F32)
    u_rows = row_derivative(u, before_ref[0].astype(F32), after_ref[0].astype(F32), first, final)
    v_rows = row_derivative(v, before_ref[1].astype(F32), after_ref[1].astype(F32), first, final)
    whole_ref[0] = v_rows.astype(BF16)
    whole_ref[1] = (0.5 * (u_rows + column_derivative(v))).astype(BF16)
    scatter_columns(whole_ref, where_ref[0], outs)


def strain_blocks(kernel, where, arrays, peers, out_block):
    width = arrays[0].shape[-1]
    block = jax.ShapeDtypeStruct(out_block + (width // peers,), BF16)
    return pl.pallas_call(
        kernel,
        in_specs=[SMEM] + [VMEM] * len(arrays),
        out_specs=[VMEM] * peers,
        out_shape=[block] * peers,
        scratch_shapes=[pltpu.VMEM(out_block + (width,), BF16)],
        compiler_params=PARAMS,
        name=kernel.__name__,
    )(where, *arrays)


def upper_blocks(count):
    return [(i, j) for i in range(count) for j in range(i, count)]


def gram_kernel(where_ref, *refs, peers):
    normal, shear = refs[:peers], refs[peers:2 * peers]
    snap_ref, kept_ref, sent_ref, both_ref = refs[2 * peers:]
    frames = normal[0].shape[0]
    for shift in range(peers):
        source = lax.rem(where_ref[0] + peers - shift, peers)
        rows = pl.ds(pl.multiple_of(source * frames, frames), frames)
        snap_ref[0, rows, :] = normal[shift][...]
        snap_ref[1, rows, :] = shear[shift][0]
        snap_ref[2, rows, :] = shear[shift][1]
    pairs = upper_blocks(snap_ref.shape[1] // BLOCK)
    half = len(pairs) // 2
    for i in range(snap_ref.shape[1] // BLOCK):
        total = None
        for c in range(3):
            left = snap_ref[c, i * BLOCK:(i + 1) * BLOCK, :]
            right = snap_ref[c, i * BLOCK:, :]
            part = lax.dot_general(left, right, (((1,), (1,)), ((), ())), preferred_element_type=F32)
            total = part if total is None else total + part
        for n, (row, col) in enumerate(pairs):
            if row == i:
                both_ref[n // half, n % half] = total[:, (col - i) * BLOCK:(col - i + 1) * BLOCK]
    core = where_ref[3]
    kept_ref[...] = both_ref[core]
    sent_ref[...] = both_ref[1 - core]


def cross_products(where, normal, shear):
    peers = len(normal)
    frames, width = normal[0].shape
    count = frames * peers // BLOCK
    half = count * (count + 1) // 4
    part = jax.ShapeDtypeStruct((half, BLOCK, BLOCK), F32)
    return pl.pallas_call(
        functools.partial(gram_kernel, peers=peers),
        in_specs=[SMEM] + [VMEM] * (2 * peers),
        out_specs=[VMEM] * 3,
        out_shape=[jax.ShapeDtypeStruct((3, frames * peers, width), BF16), part, part],
        scratch_shapes=[pltpu.VMEM((2, half, BLOCK, BLOCK), F32)],
        compiler_params=PARAMS,
        name="gram_kernel",
    )(where, *normal, *shear)


def eliminate_block(rows):
    tiles = len(rows)
    lane = lax.broadcasted_iota(jnp.int32, (SUB, BLOCK), 1)
    sub = lax.broadcasted_iota(jnp.int32, (SUB, BLOCK), 0)
    upper, inverse = [], []
    rows = list(rows)
    for step in range(tiles):
        base = step * SUB
        block = rows[step]
        a = {}
        for j in range(SUB):
            column = jnp.broadcast_to(block[:, base + j:base + j + 1], (SUB, BLOCK))
            for i in range(j, SUB):
                a[i, j] = jnp.broadcast_to(column[i:i + 1, :], (SUB, BLOCK))
        inside = (lane >= base) & (lane < base + SUB)
        seeded = jnp.where(inside, (lane - base == sub).astype(F32), block)
        v = [jnp.broadcast_to(seeded[i:i + 1, :], (SUB, BLOCK)) for i in range(SUB)]
        unit = {}
        pivot, root = [], []
        for j in range(SUB):
            inv = 1.0 / a[j, j]
            pivot.append(inv)
            root.append(lax.rsqrt(a[j, j]))
            for i in range(j + 1, SUB):
                unit[i, j] = a[i, j] * inv
            for m in range(j + 1, SUB):
                for i in range(m, SUB):
                    a[i, m] = a[i, m] - (a[i, j] * a[m, j]) * inv
            for i in range(j + 1, SUB):
                v[i] = v[i] - unit[i, j] * v[j]
        z = [v[j] * pivot[j] for j in range(SUB)]
        done = jnp.zeros((SUB, BLOCK), F32)
        corner = jnp.zeros((SUB, BLOCK), F32)
        for i in range(SUB):
            line = jnp.zeros((SUB, BLOCK), F32)
            for m in range(i, SUB):
                line = jnp.where(lane == base + m, a[m, i], line)
            done = jnp.where(sub == i, v[i] * root[i], done)
            corner = jnp.where(sub == i, line * root[i], corner)
        upper.append(jnp.where(lane >= base + SUB, done, corner))
        inverse.append(jnp.where(lane < base + SUB, done, 0.0))
        for q in range(step + 1, tiles):
            old = rows[q]
            acc = jnp.where(inside, 0.0, old)
            left = [jnp.broadcast_to(old[:, base + j:base + j + 1], (SUB, BLOCK)) for j in range(SUB)]
            for j in range(SUB):
                for m in range(j + 1, SUB):
                    left[m] = left[m] - left[j] * unit[m, j]
                acc = acc - left[j] * z[j]
            rows[q] = acc
    return upper, inverse


def span(k):
    return slice(k * BLOCK, (k + 1) * BLOCK)


def factor_kernel(where_ref, kept_ref, other_ref, factor_ref, hi_ref, lo_ref, both_ref, m_ref, t_ref, *, scale):
    n = m_ref.shape[0]
    blocks = n // BLOCK
    core = where_ref[3]
    both_ref[core] = kept_ref[...]
    both_ref[1 - core] = other_ref[...]
    pairs = upper_blocks(blocks)
    half = len(pairs) // 2
    for k in range(1, blocks):
        m_ref[span(k), :k * BLOCK] = jnp.zeros((BLOCK, k * BLOCK), F32)
    for index, (row, col) in enumerate(pairs):
        m_ref[span(row), span(col)] = both_ref[index // half, index % half]
    for k in range(blocks):
        rows = [m_ref[k * BLOCK + s:k * BLOCK + s + SUB, span(k)] for s in range(0, BLOCK, SUB)]
        upper, inverse = eliminate_block(rows)
        for s in range(BLOCK // SUB):
            t_ref[s * SUB:(s + 1) * SUB, :] = inverse[s]
            factor_ref[k * BLOCK + s * SUB:k * BLOCK + (s + 1) * SUB, span(k)] = upper[s] * (1.0 / scale)
        t = t_ref[...]
        m_ref[span(k), :] = lax.dot_general(t, m_ref[span(k), :], (((1,), (0,)), ((), ())), precision=HIGH, preferred_element_type=F32)
        m_ref[span(k), span(k)] = t
        rest = n - (k + 1) * BLOCK
        if rest:
            panel = m_ref[span(k), :]
            below = slice((k + 1) * BLOCK, n)
            m_ref[below, span(k)] = jnp.zeros((rest, BLOCK), F32)
            m_ref[below, :] = m_ref[below, :] - lax.dot_general(panel[:, (k + 1) * BLOCK:], panel, (((0,), (0,)), ((), ())), precision=HIGH, preferred_element_type=F32)
    col = lax.broadcasted_iota(jnp.int32, (BLOCK, n), 1)
    for k in range(blocks):
        whole = m_ref[span(k), :]
        if k + 1 < blocks:
            factor_ref[span(k), (k + 1) * BLOCK:] = whole[:, (k + 1) * BLOCK:] * (1.0 / scale)
        if k:
            factor_ref[span(k), :k * BLOCK] = jnp.zeros((BLOCK, k * BLOCK), F32)
        inv = jnp.where(col < (k + 1) * BLOCK, whole, 0.0) * scale
        hi = inv.astype(BF16)
        hi_ref[span(k), :] = hi
        lo_ref[span(k), :] = (inv - hi.astype(F32)).astype(BF16)


def factorize(where, kept, other, n, scale):
    return pl.pallas_call(
        functools.partial(factor_kernel, scale=scale),
        in_specs=[SMEM, VMEM, VMEM],
        out_specs=[VMEM] * 3,
        out_shape=[jax.ShapeDtypeStruct((n, n), F32)] + [jax.ShapeDtypeStruct((n, n), BF16)] * 2,
        scratch_shapes=[pltpu.VMEM((2,) + kept.shape, F32), pltpu.VMEM((n, n), F32), pltpu.VMEM((BLOCK, BLOCK), F32)],
        compiler_params=PARAMS,
        name="factor_kernel",
    )(where, kept, other)


def basis_kernel(hi_ref, lo_ref, snap_ref, out_ref):
    n = hi_ref.shape[0]
    chunk = n // 2
    for r in range(2):
        rows, depth = slice(r * chunk, (r + 1) * chunk), (r + 1) * chunk
        part = snap_ref[0, :depth, :]
        total = jnp.dot(hi_ref[rows, :depth], part, preferred_element_type=F32)
        total = total + jnp.dot(lo_ref[rows, :depth], part, preferred_element_type=F32)
        out_ref[0, rows, :] = total.astype(BF16)


def make_basis(hi, lo, snap):
    block = pl.BlockSpec((1,) + snap.shape[1:], lambda c: (c, 0, 0))
    return pl.pallas_call(
        basis_kernel,
        grid=(snap.shape[0],),
        in_specs=[VMEM, VMEM, block],
        out_specs=block,
        out_shape=jax.ShapeDtypeStruct(snap.shape, BF16),
        compiler_params=PARAMS,
        name="basis_kernel",
    )(hi, lo, snap)


def exchange(blocks, axis):
    peers = len(blocks)
    received = [blocks[0]]
    for shift in range(1, peers):
        received.append(lax.ppermute(blocks[shift], axis, [(i, (i + shift) % peers) for i in range(peers)]))
    return received


def sum_devices(kept, sent):
    swap = [(0, 1), (1, 0)]
    shape = kept.shape
    kept = (kept + lax.ppermute(sent, "core", swap)).reshape(-1, shape[-1])
    plane = lax.axis_size(("x", "y"))
    part, width = kept.shape[0] // plane, kept.shape[1]
    piece = lax.all_to_all(kept.reshape(plane, part, width), ("x", "y"), 0, 0, tiled=True).sum(0)
    copies = jnp.broadcast_to(piece[None], (lax.axis_size("z"), part, width))
    piece = lax.all_to_all(copies, "z", 0, 0, tiled=True).sum(0)
    copies = jnp.broadcast_to(piece[None], (plane, part, width))
    kept = lax.all_to_all(copies, ("x", "y"), 0, 0, tiled=True).reshape(shape)
    return kept, lax.ppermute(kept, "core", swap)


def local(displacement):
    frames, _, _, width = displacement.shape
    peers = lax.axis_size("z")
    total_rows = lax.axis_size(TILE)
    total_frames = frames * peers
    scale = math.sqrt(3 * total_rows * width)
    where = jnp.stack([lax.axis_index("z"), lax.axis_index(TILE), jnp.int32(total_rows), lax.axis_index("core")]).astype(jnp.int32)
    planes = displacement.reshape(frames, 2, width).transpose(1, 0, 2)
    up = [(i, i + 1) for i in range(total_rows - 1)]
    before = lax.ppermute(planes, TILE, up)
    after = lax.ppermute(planes, TILE, [(j, i) for i, j in up])
    normal = exchange(strain_blocks(normal_kernel, where, [planes], peers, (frames,)), "z")
    shear = exchange(strain_blocks(shear_kernel, where, [planes, before, after], peers, (2, frames)), "z")
    snap, kept, sent = cross_products(where, normal, shear)
    kept, other = sum_devices(kept, sent)
    factor, hi, lo = factorize(where, kept, other, total_frames, scale)
    basis = make_basis(hi, lo, snap)
    return basis.transpose(1, 0, 2)[:, :, None, :], factor


def solution(mesh):
    frames, tiles = mesh.devices.shape
    side = math.isqrt(tiles // 2)
    split = Mesh(mesh.devices.reshape(frames, side, side, 2), ("z",) + TILE)
    return jax.shard_map(
        local,
        mesh=split,
        in_specs=(P("z", None, TILE, None),),
        out_specs=(P(None, None, TILE, "z"), P()),
        check_vma=False,
    )
```

time: 532 us -> 141 us (0.27); the launches traced: 526 us -> 141 us
  waiting for transfers between devices: 272 us -> 22.6 us
  other arithmetic: 127 us -> 0.15 us
  local copies, waits for them, and re-layouts: 48 us -> 1.84 us
  starting transfers between devices: 6.55 us -> 43.3 us
  Pallas kernels: 0 us -> 29.4 us
  matrix products: 17.9 us -> 0 us
  between operations: 17.1 us -> 0.73 us
  blocking collectives: 37.4 us -> 43.1 us
    psum x1 -> x0, waiting for transfers between devices: 258 us -> none  [local(): gram = lax.psum(local_gram, ('frame', 'tile'))]
    another operation x19 -> x1, other arithmetic: 120 us -> 0.08 us  [local(): jnp.stack([lax.axis_index('z'), lax.axis_index(TILE), jnp.int32(total_row...]
    ppermute x2 -> x18, starting transfers between devices: 6.52 us -> 43.3 us  [the longest x14 31.8 us: exchange(): lax.ppermute(blocks[shift], axis, [(i, (i + shift) % peers) for i in rang...]
    pallas_call x0 -> x5, Pallas kernels: none -> 29.4 us  [the longest x1 22.2 us: factorize(): pl.pallas_call(functools.partial(factor_kernel, scale=scale), in_specs=[S...]
    another operation x27 -> x0, local copies, waits for them, and re-layouts: 24.3 us -> none
    another operation x13 -> x0, matrix products: 16 us -> none  [the longest x7 14.1 us: local(): lax.linalg.triangular_solve(lower, snapshot, left_side=True, lower=True)]
    unnamed x16 -> x1, local copies, waits for them, and re-layouts: 15.4 us -> 1.81 us
    ppermute x2 -> x18, waiting for transfers between devices: 14.2 us -> 22.6 us  [the longest x14 18.3 us: exchange(): lax.ppermute(blocks[shift], axis, [(i, (i + shift) % peers) for i in rang...]
  transfers between devices with their start and end apart: 3 -> 18, of which waited for: 3 -> 9; matrix products, arithmetic and copies ran while one was open for 1% -> 0% of each run, Pallas kernels for 0% -> 2%
where the time goes in v1:
time: 141 us
  starting transfers between devices  43.3 us (31%)
  blocking collectives  43.1 us (31%)
  Pallas kernels  29.4 us (21%)
  waiting for transfers between devices  22.6 us (16%)
  local copies, waits for them, and re-layouts  1.84 us (1%)
    ppermute x14, starting transfers between devices, exchange(): lax.ppermute(blocks[shift], axis, [(i, (i + shift) % peers) for i in rang...  31.8 us
    pallas_call x1, Pallas kernels, factorize(): pl.pallas_call(functools.partial(factor_kernel, scale=scale), in_specs=[S...  22.2 us
    all_to_all x1, blocking collectives, sum_devices(): lax.all_to_all(kept.reshape(plane, part, width), ('x', 'y'), 0, 0, tiled=...  20.4 us
    ppermute x14, waiting for transfers between devices, exchange(): lax.ppermute(blocks[shift], axis, [(i, (i + shift) % peers) for i in rang...  18.3 us
    all_to_all x1, blocking collectives, sum_devices(): kept = lax.all_to_all(copies, ('x', 'y'), 0, 0, tiled=True).reshape(shape)  11.5 us
    all_to_all x1, blocking collectives, sum_devices(): piece = lax.all_to_all(copies, 'z', 0, 0, tiled=True).sum(0)  11.2 us
    ppermute x1, starting transfers between devices, local(): after = lax.ppermute(planes, TILE, [(j, i) for i, j in up])  5.15 us
    ppermute x1, starting transfers between devices, sum_devices(): return (kept, lax.ppermute(kept, 'core', swap))  4.32 us
  transfers between devices with their start and end apart: 18, of which 9 were waited for; matrix products, arithmetic and copies ran while one was open for 0% of the time, Pallas kernels for 2%

profile of v1, /device:TPU:1, one launch (start us, length us, event | category | flops | bytes accessed | tf_op | source)
XLA Modules:
  0.0 141.0 jit_solution(8338812121226266715)
XLA Ops:
  0.6 1.8 %copy.8 = bf16[64,2,1,4096]{3,0,1,2:T(8,128)(2,1)S(1)} copy(bf16[64,2,1,4096]{3,1,2,0:T(2,128)(2,1)} %param.1) | data formatting | bytes 2097152 | tf_op args[0]
  2.4 5.1 %collective-permute-start.8 = (bf16[2,64,4096]{2,1,0:T(8,128)(2,1)S(1)}, bf16[2,64,4096]{2,1,0:T(8,128)(2,1)S(1)}, u32[]{:S(2)}, u32[]{:S(2)}) collective-permute-start(bf16[2,64,4096]{2,1,0:T(8,128)(2,1)S(1)} %bitcast.15), channel_id=1, source_target_pairs={{1,0},{2,1},{3,2},{4,3},{5,4},{6,5},{7,6},{8,7},{9,8},{10,9},{11,1... | collective-permute-start | bytes 3145736 | tf_op jit(solution)/shard_map/ppermute | solution.py:289
  7.6 1.9 %collective-permute-start.7 = (bf16[2,64,4096]{2,1,0:T(8,128)(2,1)S(1)}, bf16[2,64,4096]{2,1,0:T(8,128)(2,1)S(1)}, u32[]{:S(2)}, u32[]{:S(2)}) collective-permute-start(bf16[2,64,4096]{2,1,0:T(8,128)(2,1)S(1)} %bitcast.16), channel_id=1, source_target_pairs={{0,1},{1,2},{2,3},{3,4},{4,5},{5,6},{6,7},{7,8},{8,9},{9,10},{10,1... | collective-permute-start | bytes 3145736 | tf_op jit(solution)/shard_map/ppermute | solution.py:288
  9.5 0.1 pad_add_fusion.where_ref
  9.6 0.9 normal_kernel.1
  10.6 1.2 collective-permute-start
  11.7 3.0 %collective-permute-start.1 = (bf16[64,512]{1,0:T(8,128)(2,1)S(1)}, bf16[64,512]{1,0:T(8,128)(2,1)S(1)}, u32[]{:S(2)}, u32[]{:S(2)}) collective-permute-start(bf16[64,512]{1,0:T(8,128)(2,1)S(1)} %get-tuple-element.26), channel_id=1, source_target_pairs={{0,64},{32,96},{64,128},{96,160},{128,192},{160,224},{192,0},{224,... | collective-permute-start | bytes 196616 | tf_op jit(solution)/shard_map/ppermute | solution.py:261
  14.7 3.8 %collective-permute-start.2 = (bf16[64,512]{1,0:T(8,128)(2,1)S(1)}, bf16[64,512]{1,0:T(8,128)(2,1)S(1)}, u32[]{:S(2)}, u32[]{:S(2)}) collective-permute-start(bf16[64,512]{1,0:T(8,128)(2,1)S(1)} %get-tuple-element.27), channel_id=1, source_target_pairs={{0,96},{32,128},{64,160},{96,192},{128,224},{160,0},{192,32},{224,... | collective-permute-start | bytes 196616 | tf_op jit(solution)/shard_map/ppermute | solution.py:261
  18.5 1.3 collective-permute-done.8.after_ref
  19.8 6.9 %collective-permute-start.3 = (bf16[64,512]{1,0:T(8,128)(2,1)S(1)}, bf16[64,512]{1,0:T(8,128)(2,1)S(1)}, u32[]{:S(2)}, u32[]{:S(2)}) collective-permute-start(bf16[64,512]{1,0:T(8,128)(2,1)S(1)} %get-tuple-element.28), channel_id=1, source_target_pairs={{0,128},{32,160},{64,192},{96,224},{128,0},{160,32},{192,64},{224,... | collective-permute-start | bytes 196616 | tf_op jit(solution)/shard_map/ppermute | solution.py:261
  26.7 0.0 collective-permute-done.7.before_ref
  26.7 1.5 %shear_kernel.1 = (bf16[2,64,512]{2,1,0:T(8,128)(2,1)S(1)}, bf16[2,64,512]{2,1,0:T(8,128)(2,1)S(1)}, bf16[2,64,512]{2,1,0:T(8,128)(2,1)S(1)}, bf16[2,64,512]{2,1...) custom-call(s32[4]{0:T(128)S(1)} %pad_add_fusion.where_ref, ...), custom_call_target="tpu_custom_call" | custom-call | tf_op jit(solution)/shard_map/shear_kernel/pallas_call | solution.py:65
  28.2 0.8 collective-permute-start.9
  29.0 0.0 collective-permute-done.refs_1_
  29.0 1.1 collective-permute-start.10
  30.1 0.0 collective-permute-done.1.refs_2_
  30.1 3.0 %collective-permute-start.4 = (bf16[64,512]{1,0:T(8,128)(2,1)S(1)}, bf16[64,512]{1,0:T(8,128)(2,1)S(1)}, u32[]{:S(2)}, u32[]{:S(2)}) collective-permute-start(bf16[64,512]{1,0:T(8,128)(2,1)S(1)} %get-tuple-element.29), channel_id=1, source_target_pairs={{0,160},{32,192},{64,224},{96,0},{128,32},{160,64},{192,96},{224,1... | collective-permute-start | bytes 196616 | tf_op jit(solution)/shard_map/ppermute | solution.py:261
  33.1 0.0 collective-permute-done.2.refs_3_
  33.1 0.0 collective-permute-start.5
  33.1 0.0 collective-permute-done.3.refs_4_
  33.1 0.7 collective-permute-start.6
  33.8 1.9 %collective-permute-done.4.refs_5_ = bf16[64,512]{1,0:T(8,128)(2,1)S(1)} collective-permute-done((bf16[64,512]{1,0:T(8,128)(2,1)S(1)}, bf16[64,512]{1,0:T(8,128)(2,1)S(1)}, u32[]{:S(2)}, u32[]{:S(2)}) %collective-permute-start.4) | collective-permute-done | bytes 65568 | tf_op jit(solution)/shard_map/ppermute | solution.py:261
  35.7 3.7 %collective-permute-start.11 = (bf16[2,64,512]{2,1,0:T(8,128)(2,1)S(1)}, bf16[2,64,512]{2,1,0:T(8,128)(2,1)S(1)}, u32[]{:S(2)}, u32[]{:S(2)}) collective-permute-start(bf16[2,64,512]{2,1,0:T(8,128)(2,1)S(1)} %get-tuple-element.35), channel_id=1, source_target_pairs={{0,96},{32,128},{64,160},{96,192},{128,224},{160,0},{192,32},{224,... | collective-permute-start | bytes 393224 | tf_op jit(solution)/shard_map/ppermute | solution.py:261
  39.4 0.0 collective-permute-done.5.refs_6_
  39.4 3.2 %collective-permute-start.12 = (bf16[2,64,512]{2,1,0:T(8,128)(2,1)S(1)}, bf16[2,64,512]{2,1,0:T(8,128)(2,1)S(1)}, u32[]{:S(2)}, u32[]{:S(2)}) collective-permute-start(bf16[2,64,512]{2,1,0:T(8,128)(2,1)S(1)} %get-tuple-element.36), channel_id=1, source_target_pairs={{0,128},{32,160},{64,192},{96,224},{128,0},{160,32},{192,64},{224,... | collective-permute-start | bytes 393224 | tf_op jit(solution)/shard_map/ppermute | solution.py:261
  42.6 0.0 collective-permute-done.6.refs_7_
  42.6 0.3 collective-permute-start.13
  42.9 0.0 collective-permute-done.9.refs_9_
  42.9 4.0 %collective-permute-start.14 = (bf16[2,64,512]{2,1,0:T(8,128)(2,1)S(1)}, bf16[2,64,512]{2,1,0:T(8,128)(2,1)S(1)}, u32[]{:S(2)}, u32[]{:S(2)}) collective-permute-start(bf16[2,64,512]{2,1,0:T(8,128)(2,1)S(1)} %get-tuple-element.38), channel_id=1, source_target_pairs={{0,192},{32,224},{64,0},{96,32},{128,64},{160,96},{192,128},{224,1... | collective-permute-start | bytes 393224 | tf_op jit(solution)/shard_map/ppermute | solution.py:261
  46.9 0.0 collective-permute-done.10.refs_10_
  46.9 0.2 collective-permute-start.15
  47.1 0.1 collective-permute-done.11.refs_11_
  47.2 7.2 %collective-permute-done.12.refs_12_ = bf16[2,64,512]{2,1,0:T(8,128)(2,1)S(1)} collective-permute-done((bf16[2,64,512]{2,1,0:T(8,128)(2,1)S(1)}, bf16[2,64,512]{2,1,0:T(8,128)(2,1)S(1)}, u32[]{:S(2)}, u32[]{:S(2)}) %collective-permute-start.12) | collective-permute-done | bytes 131104 | tf_op jit(solution)/shard_map/ppermute | solution.py:261
  54.5 2.2 %collective-permute-done.13.refs_13_ = bf16[2,64,512]{2,1,0:T(8,128)(2,1)S(1)} collective-permute-done((bf16[2,64,512]{2,1,0:T(8,128)(2,1)S(1)}, bf16[2,64,512]{2,1,0:T(8,128)(2,1)S(1)}, u32[]{:S(2)}, u32[]{:S(2)}) %collective-permute-start.13) | collective-permute-done | bytes 131104 | tf_op jit(solution)/shard_map/ppermute | solution.py:261
  56.7 5.0 %collective-permute-done.14.refs_14_ = bf16[2,64,512]{2,1,0:T(8,128)(2,1)S(1)} collective-permute-done((bf16[2,64,512]{2,1,0:T(8,128)(2,1)S(1)}, bf16[2,64,512]{2,1,0:T(8,128)(2,1)S(1)}, u32[]{:S(2)}, u32[]{:S(2)}) %collective-permute-start.14) | collective-permute-done | bytes 131104 | tf_op jit(solution)/shard_map/ppermute | solution.py:261
  61.7 1.9 %collective-permute-done.15.refs_15_ = bf16[2,64,512]{2,1,0:T(8,128)(2,1)S(1)} collective-permute-done((bf16[2,64,512]{2,1,0:T(8,128)(2,1)S(1)}, bf16[2,64,512]{2,1,0:T(8,128)(2,1)S(1)}, u32[]{:S(2)}, u32[]{:S(2)}) %collective-permute-start.15) | collective-permute-done | bytes 131104 | tf_op jit(solution)/shard_map/ppermute | solution.py:261
  63.6 2.0 %gram_kernel.1 = (bf16[3,512,512]{2,1,0:T(8,128)(2,1)S(1)}, f32[5,128,128]{2,1,0:T(8,128)S(1)}, f32[5,128,128]{2,1,0:T(8,128)S(1)}) custom-call(s32[4]{0:T(128)S(1)} %pad_add_fusion.where_ref, bf16[64,512]{1,0:T(8,128)(2,1)S(1)} %get-tuple-element.24.refs_0_, bf16[64,512]{1,0:T(8,128)(2,1)S(1)} %collective-permute-done.refs_1_, ...), custom_call_target="tpu_custom_call" | custom-call | tf_op jit(solution)/shard_map/gram_kernel/pallas_call | solution.py:113
  65.5 0.1 collective-permute-start.16
  65.6 1.6 %collective-permute-done.16 = f32[5,128,128]{2,1,0:T(8,128)S(1)} collective-permute-done((f32[5,128,128]{2,1,0:T(8,128)S(1)}, f32[5,128,128]{2,1,0:T(8,128)S(1)}, u32[]{:S(2)}, u32[]{:S(2)}) %collective-permute-start.16) | collective-permute-done | bytes 327712 | tf_op jit(solution)/shard_map/ppermute | solution.py:268
  67.3 20.4 %all_to_all.15 = f32[16,40,128]{2,1,0:T(8,128)S(1)} all-to-all(f32[16,40,128]{2,1,0:T(8,128)S(1)} %bitcast.22), channel_id=1, replica_groups=mesh['z'=8,'x'=4,'y'=4,'core'=2] {'x','y'}, dimensions={0} | all-to-all | bytes 655360 | tf_op jit(solution)/shard_map/all_to_all | solution.py:271
  87.7 11.2 %all_to_all.16 = f32[8,40,128]{2,1,0:T(8,128)S(1)} all-to-all(f32[8,40,128]{2,1,0:T(8,128)S(1)} %broadcast_in_dim.6), channel_id=1, replica_groups=mesh['z'=8,'x'=4,'y'=4,'core'=2] {'z'}, dimensions={0} | all-to-all | bytes 327680 | tf_op jit(solution)/shard_map/all_to_all | solution.py:273
  99.0 11.5 %all_to_all.17 = f32[16,40,128]{2,1,0:T(8,128)S(1)} all-to-all(f32[16,40,128]{2,1,0:T(8,128)S(1)} %broadcast_in_dim.7), channel_id=1, replica_groups=mesh['z'=8,'x'=4,'y'=4,'core'=2] {'x','y'}, dimensions={0} | all-to-all | bytes 655360 | tf_op jit(solution)/shard_map/all_to_all | solution.py:275
  110.5 4.3 %collective-permute-start.17 = (f32[5,128,128]{2,1,0:T(8,128)S(1)}, f32[5,128,128]{2,1,0:T(8,128)S(1)}, u32[]{:S(2)}, u32[]{:S(2)}) collective-permute-start(f32[5,128,128]{2,1,0:T(8,128)S(1)} %bitcast.19), channel_id=1, source_target_pairs={{0,1},{1,0},{2,3},{3,2},{4,5},{5,4},{6,7},{7,6},{8,9},{9,8},{10,11... | collective-permute-start | bytes 983048 | tf_op jit(solution)/shard_map/ppermute | solution.py:276
  114.8 1.3 collective-permute-done.17.other_ref
  116.0 22.2 %factor_kernel.1 = (f32[512,512]{1,0:T(8,128)}, bf16[512,512]{1,0:T(8,128)(2,1)S(1)}, bf16[512,512]{1,0:T(8,128)(2,1)S(1)}) custom-call(s32[4]{0:T(128)S(1)} %pad_add_fusion.where_ref, f32[5,128,128]{2,1,0:T(8,128)S(1)} %bitcast.20, f32[5,128,128]{2,1,0:T(8,128)S(1)} %collective-permute-done.17.other_ref), custom_call_target="tpu_custom_call" | custom-call | tf_op jit(solution)/shard_map/factor_kernel/pallas_call | solution.py:222
  138.3 2.7 %basis_kernel.1 = bf16[3,512,512]{2,1,0:T(8,128)(2,1)} custom-call(bf16[512,512]{1,0:T(8,128)(2,1)S(1)} %get-tuple-element.42.hi_ref, bf16[512,512]{1,0:T(8,128)(2,1)S(1)} %get-tuple-element.43.lo_ref, bf16[3,512,512]{2,1,0:T(8,128)(2,1)S(1)} %get-tuple-element.44.snap_ref), custom_call_target="tpu_custom_call" | custom-call | tf_op jit(solution)/shard_map/basis_kernel/pallas_call | solution.py:246
  (5 shorter events, 0.1 us)
Async XLA Ops:
  2.4 17.4 %collective-permute-start.8 = (bf16[2,64,4096]{2,1,0:T(8,128)(2,1)S(1)}, bf16[2,64,4096]{2,1,0:T(8,128)(2,1)S(1)}, u32[]{:S(2)}, u32[]{:S(2)}) collective-permute-start(bf16[2,64,4096]{2,1,0:T(8,128)(2,1)S(1)} %bitcast.15), channel_id=1, source_target_pairs={{1,0},{2,1},{3,2},{4,3},{5,4},{6,5},{7,6},{8,7},{9,8},{10,9},{11,1... | collective-permute-start | bytes 3145736 | tf_op jit(solution)/shard_map/ppermute | solution.py:289
  7.6 19.1 %collective-permute-start.7 = (bf16[2,64,4096]{2,1,0:T(8,128)(2,1)S(1)}, bf16[2,64,4096]{2,1,0:T(8,128)(2,1)S(1)}, u32[]{:S(2)}, u32[]{:S(2)}) collective-permute-start(bf16[2,64,4096]{2,1,0:T(8,128)(2,1)S(1)} %bitcast.16), channel_id=1, source_target_pairs={{0,1},{1,2},{2,3},{3,4},{4,5},{5,6},{6,7},{7,8},{8,9},{9,10},{10,1... | collective-permute-start | bytes 3145736 | tf_op jit(solution)/shard_map/ppermute | solution.py:288
  10.6 18.5 %collective-permute-start = (bf16[64,512]{1,0:T(8,128)(2,1)S(1)}, bf16[64,512]{1,0:T(8,128)(2,1)S(1)}, u32[]{:S(2)}, u32[]{:S(2)}) collective-permute-start(bf16[64,512]{1,0:T(8,128)(2,1)S(1)} %get-tuple-element.25), channel_id=1, source_target_pairs={{0,32},{32,64},{64,96},{96,128},{128,160},{160,192},{192,224},{224... | collective-permute-start | bytes 196616 | tf_op jit(solution)/shard_map/ppermute | solution.py:261
  11.7 18.4 %collective-permute-start.1 = (bf16[64,512]{1,0:T(8,128)(2,1)S(1)}, bf16[64,512]{1,0:T(8,128)(2,1)S(1)}, u32[]{:S(2)}, u32[]{:S(2)}) collective-permute-start(bf16[64,512]{1,0:T(8,128)(2,1)S(1)} %get-tuple-element.26), channel_id=1, source_target_pairs={{0,64},{32,96},{64,128},{96,160},{128,192},{160,224},{192,0},{224,... | collective-permute-start | bytes 196616 | tf_op jit(solution)/shard_map/ppermute | solution.py:261
  14.7 18.3 %collective-permute-start.2 = (bf16[64,512]{1,0:T(8,128)(2,1)S(1)}, bf16[64,512]{1,0:T(8,128)(2,1)S(1)}, u32[]{:S(2)}, u32[]{:S(2)}) collective-permute-start(bf16[64,512]{1,0:T(8,128)(2,1)S(1)} %get-tuple-element.27), channel_id=1, source_target_pairs={{0,96},{32,128},{64,160},{96,192},{128,224},{160,0},{192,32},{224,... | collective-permute-start | bytes 196616 | tf_op jit(solution)/shard_map/ppermute | solution.py:261
  19.8 13.3 %collective-permute-start.3 = (bf16[64,512]{1,0:T(8,128)(2,1)S(1)}, bf16[64,512]{1,0:T(8,128)(2,1)S(1)}, u32[]{:S(2)}, u32[]{:S(2)}) collective-permute-start(bf16[64,512]{1,0:T(8,128)(2,1)S(1)} %get-tuple-element.28), channel_id=1, source_target_pairs={{0,128},{32,160},{64,192},{96,224},{128,0},{160,32},{192,64},{224,... | collective-permute-start | bytes 196616 | tf_op jit(solution)/shard_map/ppermute | solution.py:261
  28.2 14.7 %collective-permute-start.9 = (bf16[2,64,512]{2,1,0:T(8,128)(2,1)S(1)}, bf16[2,64,512]{2,1,0:T(8,128)(2,1)S(1)}, u32[]{:S(2)}, u32[]{:S(2)}) collective-permute-start(bf16[2,64,512]{2,1,0:T(8,128)(2,1)S(1)} %get-tuple-element.33), channel_id=1, source_target_pairs={{0,32},{32,64},{64,96},{96,128},{128,160},{160,192},{192,224},{224... | collective-permute-start | bytes 393224 | tf_op jit(solution)/shard_map/ppermute | solution.py:261
  29.0 17.8 %collective-permute-start.10 = (bf16[2,64,512]{2,1,0:T(8,128)(2,1)S(1)}, bf16[2,64,512]{2,1,0:T(8,128)(2,1)S(1)}, u32[]{:S(2)}, u32[]{:S(2)}) collective-permute-start(bf16[2,64,512]{2,1,0:T(8,128)(2,1)S(1)} %get-tuple-element.34), channel_id=1, source_target_pairs={{0,64},{32,96},{64,128},{96,160},{128,192},{160,224},{192,0},{224,... | collective-permute-start | bytes 393224 | tf_op jit(solution)/shard_map/ppermute | solution.py:261
  30.1 5.6 %collective-permute-start.4 = (bf16[64,512]{1,0:T(8,128)(2,1)S(1)}, bf16[64,512]{1,0:T(8,128)(2,1)S(1)}, u32[]{:S(2)}, u32[]{:S(2)}) collective-permute-start(bf16[64,512]{1,0:T(8,128)(2,1)S(1)} %get-tuple-element.29), channel_id=1, source_target_pairs={{0,160},{32,192},{64,224},{96,0},{128,32},{160,64},{192,96},{224,1... | collective-permute-start | bytes 196616 | tf_op jit(solution)/shard_map/ppermute | solution.py:261
  33.1 6.4 %collective-permute-start.5 = (bf16[64,512]{1,0:T(8,128)(2,1)S(1)}, bf16[64,512]{1,0:T(8,128)(2,1)S(1)}, u32[]{:S(2)}, u32[]{:S(2)}) collective-permute-start(bf16[64,512]{1,0:T(8,128)(2,1)S(1)} %get-tuple-element.30), channel_id=1, source_target_pairs={{0,192},{32,224},{64,0},{96,32},{128,64},{160,96},{192,128},{224,1... | collective-permute-start | bytes 196616 | tf_op jit(solution)/shard_map/ppermute | solution.py:261
  33.1 9.5 %collective-permute-start.6 = (bf16[64,512]{1,0:T(8,128)(2,1)S(1)}, bf16[64,512]{1,0:T(8,128)(2,1)S(1)}, u32[]{:S(2)}, u32[]{:S(2)}) collective-permute-start(bf16[64,512]{1,0:T(8,128)(2,1)S(1)} %get-tuple-element.31), channel_id=1, source_target_pairs={{0,224},{32,0},{64,32},{96,64},{128,96},{160,128},{192,160},{224,1... | collective-permute-start | bytes 196616 | tf_op jit(solution)/shard_map/ppermute | solution.py:261
  35.7 11.5 %collective-permute-start.11 = (bf16[2,64,512]{2,1,0:T(8,128)(2,1)S(1)}, bf16[2,64,512]{2,1,0:T(8,128)(2,1)S(1)}, u32[]{:S(2)}, u32[]{:S(2)}) collective-permute-start(bf16[2,64,512]{2,1,0:T(8,128)(2,1)S(1)} %get-tuple-element.35), channel_id=1, source_target_pairs={{0,96},{32,128},{64,160},{96,192},{128,224},{160,0},{192,32},{224,... | collective-permute-start | bytes 393224 | tf_op jit(solution)/shard_map/ppermute | solution.py:261
  39.4 15.1 %collective-permute-start.12 = (bf16[2,64,512]{2,1,0:T(8,128)(2,1)S(1)}, bf16[2,64,512]{2,1,0:T(8,128)(2,1)S(1)}, u32[]{:S(2)}, u32[]{:S(2)}) collective-permute-start(bf16[2,64,512]{2,1,0:T(8,128)(2,1)S(1)} %get-tuple-element.36), channel_id=1, source_target_pairs={{0,128},{32,160},{64,192},{96,224},{128,0},{160,32},{192,64},{224,... | collective-permute-start | bytes 393224 | tf_op jit(solution)/shard_map/ppermute | solution.py:261
  42.6 14.1 %collective-permute-start.13 = (bf16[2,64,512]{2,1,0:T(8,128)(2,1)S(1)}, bf16[2,64,512]{2,1,0:T(8,128)(2,1)S(1)}, u32[]{:S(2)}, u32[]{:S(2)}) collective-permute-start(bf16[2,64,512]{2,1,0:T(8,128)(2,1)S(1)} %get-tuple-element.37), channel_id=1, source_target_pairs={{0,160},{32,192},{64,224},{96,0},{128,32},{160,64},{192,96},{224,1... | collective-permute-start | bytes 393224 | tf_op jit(solution)/shard_map/ppermute | solution.py:261
  42.9 18.8 %collective-permute-start.14 = (bf16[2,64,512]{2,1,0:T(8,128)(2,1)S(1)}, bf16[2,64,512]{2,1,0:T(8,128)(2,1)S(1)}, u32[]{:S(2)}, u32[]{:S(2)}) collective-permute-start(bf16[2,64,512]{2,1,0:T(8,128)(2,1)S(1)} %get-tuple-element.38), channel_id=1, source_target_pairs={{0,192},{32,224},{64,0},{96,32},{128,64},{160,96},{192,128},{224,1... | collective-permute-start | bytes 393224 | tf_op jit(solution)/shard_map/ppermute | solution.py:261
  46.9 16.7 %collective-permute-start.15 = (bf16[2,64,512]{2,1,0:T(8,128)(2,1)S(1)}, bf16[2,64,512]{2,1,0:T(8,128)(2,1)S(1)}, u32[]{:S(2)}, u32[]{:S(2)}) collective-permute-start(bf16[2,64,512]{2,1,0:T(8,128)(2,1)S(1)} %get-tuple-element.39), channel_id=1, source_target_pairs={{0,224},{32,0},{64,32},{96,64},{128,96},{160,128},{192,160},{224,1... | collective-permute-start | bytes 393224 | tf_op jit(solution)/shard_map/ppermute | solution.py:261
  65.5 1.7 %collective-permute-start.16 = (f32[5,128,128]{2,1,0:T(8,128)S(1)}, f32[5,128,128]{2,1,0:T(8,128)S(1)}, u32[]{:S(2)}, u32[]{:S(2)}) collective-permute-start(f32[5,128,128]{2,1,0:T(8,128)S(1)} %get-tuple-element.41), channel_id=1, source_target_pairs={{0,1},{1,0},{2,3},{3,2},{4,5},{5,4},{6,7},{7,6},{8,9},{9,8},{10,11... | collective-permute-start | bytes 983048 | tf_op jit(solution)/shard_map/ppermute | solution.py:268
  110.5 5.6 %collective-permute-start.17 = (f32[5,128,128]{2,1,0:T(8,128)S(1)}, f32[5,128,128]{2,1,0:T(8,128)S(1)}, u32[]{:S(2)}, u32[]{:S(2)}) collective-permute-start(f32[5,128,128]{2,1,0:T(8,128)S(1)} %bitcast.19), channel_id=1, source_target_pairs={{0,1},{1,0},{2,3},{3,2},{4,5},{5,4},{6,7},{7,6},{8,9},{9,8},{10,11... | collective-permute-start | bytes 983048 | tf_op jit(solution)/shard_map/ppermute | solution.py:276

commit v2 on v1

--- a/solution.py
+++ b/solution.py
@@ -11,21 +11,106 @@
 TILE = ("x", "y", "core")
 SUB = 8
 BLOCK = 128
+LANES = 128
 HIGH = lax.Precision.HIGHEST
 F32 = jnp.float32
 BF16 = jnp.bfloat16
 VMEM = pl.BlockSpec(memory_space=pltpu.VMEM)
 SMEM = pl.BlockSpec(memory_space=pltpu.SMEM)
-PARAMS = pltpu.CompilerParams(vmem_limit_bytes=40 << 20)
-
-
-def column_derivative(center):
-    width = center.shape[-1]
-    column = lax.broadcasted_iota(jnp.int32, center.shape, center.ndim - 1)
-    first, final = column == 0, column == width - 1
-    after = jnp.where(final, center, pltpu.roll(center, width - 1, center.ndim - 1))
-    before = jnp.where(first, center, pltpu.roll(center, 1, center.ndim - 1))
-    return (after - before) * jnp.where(first | final, 1.0, 0.5)
+PARAMS = pltpu.CompilerParams(vmem_limit_bytes=24 << 20)
+
+
+def turns(sign):
+    return [0, 2 * sign, -3, 3, -2 * sign, 4, -1, 1]
+
+
+def spread_kernel(where_ref, planes_ref, *outs):
+    place, core = where_ref[0], where_ref[3]
+    own_ref, pair_ref = outs[0], outs[1]
+    singles = dict(zip((2, 3, 4, 6, 7), outs[2:]))
+    width = own_ref.shape[1]
+    fields, frames, total = planes_ref.shape
+    peers = total // width
+    rows = fields * frames
+    row = lax.broadcasted_iota(jnp.int32, (SUB, LANES), 0)
+    lane = lax.broadcasted_iota(jnp.int32, (SUB, LANES), 1)
+    last = ((row == 0) & (lane == LANES - 1)).astype(BF16)
+    first = ((row == 1) & (lane == 0)).astype(BF16)
+    for slot, offset in enumerate(turns(1 - 2 * core)):
+        out_ref = own_ref if slot == 0 else pair_ref.at[0] if slot == 1 else pair_ref.at[1] if slot == 5 else singles[slot]
+        start = lax.rem(place + offset + peers, peers) * width
+        left = pl.multiple_of(jnp.maximum(start - LANES, 0), LANES)
+        right = pl.multiple_of(jnp.minimum(start + width, total - LANES), LANES)
+        out_ref[rows:, :] = jnp.zeros((SUB, width), BF16)
+        for field in range(fields):
+            part = slice(field * frames, (field + 1) * frames)
+            out_ref[part, :] = planes_ref[field, :, pl.ds(pl.multiple_of(start, width), width)]
+        below = planes_ref[:, :, pl.ds(left, LANES)].reshape(rows, LANES)
+        above = planes_ref[:, :, pl.ds(right, LANES)].reshape(rows, LANES)
+        dims = (((1,), (1,)), ((), ()))
+        edges = lax.dot_general(last, below, dims, preferred_element_type=F32)
+        edges = edges + lax.dot_general(first, above, dims, preferred_element_type=F32)
+        out_ref[rows:, :rows] = edges.astype(BF16)
+
+
+def spread(where, planes, peers):
+    fields, frames, width = planes.shape
+    block = jax.ShapeDtypeStruct((fields * frames + SUB, width // peers), BF16)
+    pair = jax.ShapeDtypeStruct((2,) + block.shape, BF16)
+    return pl.pallas_call(
+        spread_kernel,
+        in_specs=[SMEM, VMEM],
+        out_specs=[VMEM] * 7,
+        out_shape=[block, pair] + [block] * 5,
+        compiler_params=PARAMS,
+        name="spread_kernel",
+    )(where, planes)
+
+
+def collect_kernel(*refs):
+    blocks, out_ref = refs[:-1], refs[-1]
+    slot = 0
+    for block in blocks:
+        if len(block.shape) == 3:
+            out_ref[slot] = block[0]
+        else:
+            out_ref[slot] = block[...]
+        slot += 1
+
+
+def collect(*blocks):
+    return pl.pallas_call(
+        collect_kernel,
+        in_specs=[VMEM] * len(blocks),
+        out_specs=VMEM,
+        out_shape=jax.ShapeDtypeStruct((len(blocks),) + blocks[0].shape, BF16),
+        compiler_params=PARAMS,
+        name="collect_kernel",
+    )(*blocks)
+
+
+def shifted(block, near, far, peers):
+    pairs = []
+    for i in range(peers):
+        pairs += [(2 * i, 2 * ((i + near) % peers)), (2 * i + 1, 2 * ((i + far) % peers) + 1)]
+    return lax.ppermute(block, ("z", "core"), pairs)
+
+
+def exchange(where, planes, peers):
+    own, pair, minus3, plus3, back2, minus1, plus1 = spread(where, planes, peers)
+    pair = shifted(pair, 2, -2, peers)
+    minus3 = shifted(minus3, -3, -3, peers)
+    plus3 = shifted(plus3, 3, 3, peers)
+    first = collect(own, pair, minus3, plus3)
+    back2 = shifted(back2, -2, 2, peers)
+    relayed = shifted(pair[1], 2, -2, peers)
+    minus1 = shifted(minus1, -1, -1, peers)
+    plus1 = shifted(plus1, 1, 1, peers)
+    second = collect(back2, relayed, minus1, plus1)
+    return first, second
+
+
+NEXT = (0, 4, 2, 3, 1, 5, 6, 7)
 
 
 def row_derivative(center, before, after, first, final):
@@ -34,91 +119,84 @@
     return (after - before) * jnp.where(first | final, 1.0, 0.5)
 
 
-def scatter_columns(whole_ref, place, outs):
-    peers = len(outs)
-    width = outs[0].shape[-1]
-    for shift in range(peers):
-        start = pl.multiple_of(lax.rem(place + shift, peers) * width, width)
-        outs[shift][...] = whole_ref[..., pl.ds(start, width)]
-
-
-def normal_kernel(where_ref, center_ref, *refs):
-    outs, whole_ref = refs[:-1], refs[-1]
-    whole_ref[...] = column_derivative(center_ref[0].astype(F32)).astype(BF16)
-    scatter_columns(whole_ref, where_ref[0], outs)
-
-
-def shear_kernel(where_ref, center_ref, before_ref, after_ref, *refs):
-    outs, whole_ref = refs[:-1], refs[-1]
-    first, final = where_ref[1] == 0, where_ref[1] == where_ref[2] - 1
-    u, v = center_ref[0].astype(F32), center_ref[1].astype(F32)
-    u_rows = row_derivative(u, before_ref[0].astype(F32), after_ref[0].astype(F32), first, final)
-    v_rows = row_derivative(v, before_ref[1].astype(F32), after_ref[1].astype(F32), first, final)
-    whole_ref[0] = v_rows.astype(BF16)
-    whole_ref[1] = (0.5 * (u_rows + column_derivative(v))).astype(BF16)
-    scatter_columns(whole_ref, where_ref[0], outs)
-
-
-def strain_blocks(kernel, where, arrays, peers, out_block):
-    width = arrays[0].shape[-1]
-    block = jax.ShapeDtypeStruct(out_block + (width // peers,), BF16)
-    return pl.pallas_call(
-        kernel,
-        in_specs=[SMEM] + [VMEM] * len(arrays),
-        out_specs=[VMEM] * peers,
-        out_shape=[block] * peers,
-        scratch_shapes=[pltpu.VMEM(out_block + (width,), BF16)],
-        compiler_params=PARAMS,
-        name=kernel.__name__,
-    )(where, *arrays)
+def column_derivative(center, left, right, start, total):
+    width = center.shape[1]
+    lane = lax.broadcasted_iota(jnp.int32, center.shape, 1)
+    column = lane + start
+    first, final = column == 0, column == total - 1
+    before = jnp.where(lane == 0, left, pltpu.roll(center, 1, 1))
+    after = jnp.where(lane == width - 1, right, pltpu.roll(center, width - 1, 1))
+    after = jnp.where(final, center, after)
+    before = jnp.where(first, center, before)
+    return (after - before) * jnp.where(first | final, 1.0, 0.5)
 
 
 def upper_blocks(count):
     return [(i, j) for i in range(count) for j in range(i, count)]
 
 
-def gram_kernel(where_ref, *refs, peers):
-    normal, shear = refs[:peers], refs[peers:2 * peers]
-    snap_ref, kept_ref, sent_ref, both_ref = refs[2 * peers:]
-    frames = normal[0].shape[0]
-    for shift in range(peers):
-        source = lax.rem(where_ref[0] + peers - shift, peers)
-        rows = pl.ds(pl.multiple_of(source * frames, frames), frames)
-        snap_ref[0, rows, :] = normal[shift][...]
-        snap_ref[1, rows, :] = shear[shift][0]
-        snap_ref[2, rows, :] = shear[shift][1]
-    pairs = upper_blocks(snap_ref.shape[1] // BLOCK)
+def gram_kernel(where_ref, *refs):
+    parts, snap_ref, kept_ref, sent_ref, both_ref = refs[:6], *refs[6:]
+    center, before, after = parts[0:2], parts[2:4], parts[4:6]
+    half_peers, _, width = center[0].shape
+    peers = 2 * half_peers
+    total = snap_ref.shape[1]
+    frames = total // peers
+    rows = 2 * frames
+    top, bottom = where_ref[1] == 0, where_ref[1] == where_ref[2] - 1
+    start = where_ref[0] * width
+    row = lax.broadcasted_iota(jnp.int32, (SUB, LANES), 0)
+    turn = (((0,), (0,)), ((), ()))
+    for slot, offset in enumerate(turns(1 - 2 * where_ref[3])):
+        here = center[slot // half_peers].at[slot % half_peers]
+        beside = NEXT[slot]
+        above = before[beside // half_peers].at[beside % half_peers]
+        below = after[beside // half_peers].at[beside % half_peers]
+        edges = here[rows:, :rows]
+        left = lax.dot_general(edges, (row == 0).astype(BF16), turn, preferred_element_type=F32)
+        right = lax.dot_general(edges, (row == 1).astype(BF16), turn, preferred_element_type=F32)
+        u_rows, v_rows = slice(0, frames), slice(frames, rows)
+        u, v = here[u_rows, :].astype(F32), here[v_rows, :].astype(F32)
+        slope_u = row_derivative(u, above[u_rows, :].astype(F32), below[u_rows, :].astype(F32), top, bottom)
+        slope_v = row_derivative(v, above[v_rows, :].astype(F32), below[v_rows, :].astype(F32), top, bottom)
+        along_u = column_derivative(u, left[u_rows, :1], right[u_rows, :1], start, width * peers)
+        along_v = column_derivative(v, left[v_rows, :1], right[v_rows, :1], start, width * peers)
+        source = lax.rem(where_ref[0] + peers - offset, peers)
+        lines = pl.ds(pl.multiple_of(source * frames, frames), frames)
+        snap_ref[0, lines, :] = along_u.astype(BF16)
+        snap_ref[1, lines, :] = slope_v.astype(BF16)
+        snap_ref[2, lines, :] = (0.5 * (slope_u + along_v)).astype(BF16)
+    pairs = upper_blocks(total // BLOCK)
     half = len(pairs) // 2
-    for i in range(snap_ref.shape[1] // BLOCK):
-        total = None
+    for i in range(total // BLOCK):
+        sums = None
         for c in range(3):
-            left = snap_ref[c, i * BLOCK:(i + 1) * BLOCK, :]
+            left = snap_ref[c, span(i), :]
             right = snap_ref[c, i * BLOCK:, :]
             part = lax.dot_general(left, right, (((1,), (1,)), ((), ())), preferred_element_type=F32)
-            total = part if total is None else total + part
-        for n, (row, col) in enumerate(pairs):
-            if row == i:
-                both_ref[n // half, n % half] = total[:, (col - i) * BLOCK:(col - i + 1) * BLOCK]
+            sums = part if sums is None else sums + part
+        for n, (line, col) in enumerate(pairs):
+            if line == i:
+                both_ref[n // half, n % half] = sums[:, (col - i) * BLOCK:(col - i + 1) * BLOCK]
     core = where_ref[3]
     kept_ref[...] = both_ref[core]
     sent_ref[...] = both_ref[1 - core]
 
 
-def cross_products(where, normal, shear):
-    peers = len(normal)
-    frames, width = normal[0].shape
-    count = frames * peers // BLOCK
+def cross_products(where, parts, total):
+    width = parts[0].shape[2]
+    count = total // BLOCK
     half = count * (count + 1) // 4
     part = jax.ShapeDtypeStruct((half, BLOCK, BLOCK), F32)
     return pl.pallas_call(
-        functools.partial(gram_kernel, peers=peers),
-        in_specs=[SMEM] + [VMEM] * (2 * peers),
+        gram_kernel,
+        in_specs=[SMEM] + [VMEM] * len(parts),
         out_specs=[VMEM] * 3,
-        out_shape=[jax.ShapeDtypeStruct((3, frames * peers, width), BF16), part, part],
+        out_shape=[jax.ShapeDtypeStruct((3, total, width), BF16), part, part],
         scratch_shapes=[pltpu.VMEM((2, half, BLOCK, BLOCK), F32)],
         compiler_params=PARAMS,
         name="gram_kernel",
-    )(where, *normal, *shear)
+    )(where, *parts)
 
 
 def eliminate_block(rows):
@@ -254,14 +332,6 @@
     )(hi, lo, snap)
 
 
-def exchange(blocks, axis):
-    peers = len(blocks)
-    received = [blocks[0]]
-    for shift in range(1, peers):
-        received.append(lax.ppermute(blocks[shift], axis, [(i, (i + shift) % peers) for i in range(peers)]))
-    return received
-
-
 def sum_devices(kept, sent):
     swap = [(0, 1), (1, 0)]
     shape = kept.shape
@@ -284,12 +354,12 @@
     scale = math.sqrt(3 * total_rows * width)
     where = jnp.stack([lax.axis_index("z"), lax.axis_index(TILE), jnp.int32(total_rows), lax.axis_index("core")]).astype(jnp.int32)
     planes = displacement.reshape(frames, 2, width).transpose(1, 0, 2)
+    first, second = exchange(where, planes, peers)
     up = [(i, i + 1) for i in range(total_rows - 1)]
-    before = lax.ppermute(planes, TILE, up)
-    after = lax.ppermute(planes, TILE, [(j, i) for i, j in up])
-    normal = exchange(strain_blocks(normal_kernel, where, [planes], peers, (frames,)), "z")
-    shear = exchange(strain_blocks(shear_kernel, where, [planes, before, after], peers, (2, frames)), "z")
-    snap, kept, sent = cross_products(where, normal, shear)
+    down = [(j, i) for i, j in up]
+    before = [lax.ppermute(part, TILE, up) for part in (first, second)]
+    after = [lax.ppermute(part, TILE, down) for part in (first, second)]
+    snap, kept, sent = cross_products(where, [first, second] + before + after, total_frames)
     kept, other = sum_devices(kept, sent)
     factor, hi, lo = factorize(where, kept, other, total_frames, scale)
     basis = make_basis(hi, lo, snap)

time: 141 us -> 129 us (0.915)
  waiting for transfers between devices: 22.6 us -> 11 us
    ppermute x16 -> x11, waiting for transfers between devices: 19.7 us -> 8.11 us  [the longest x2 4.78 us: local(): after = [lax.ppermute(part, TILE, down) for part in (first, second)]]
    ppermute x16 -> x11, starting transfers between devices: 38.9 us -> 39.1 us  [the longest x7 28 us: shifted(): return lax.ppermute(block, ('z', 'core'), pairs)]
    pallas_call x3 -> x4, Pallas kernels: 4.41 us -> 4.61 us  [the longest x1 3.59 us: cross_products(): pl.pallas_call(gram_kernel, in_specs=[SMEM] + [VMEM] * len(parts), out_sp...]
  transfers between devices with their start and end apart: 18 -> 13, of which waited for: 9 -> 6; matrix products, arithmetic and copies ran while one was open for 0% -> 0% of each run, Pallas kernels for 2% -> 0%
where the time goes in v2:
time: 129 us; the launch traced here: 128 us
  starting transfers between devices  43.5 us (34%)
  blocking collectives  41.7 us (32%)
  Pallas kernels  29.5 us (23%)
  waiting for transfers between devices  11 us (9%)
  local copies, waits for them, and re-layouts  1.85 us (1%)
    ppermute x7, starting transfers between devices, shifted(): return lax.ppermute(block, ('z', 'core'), pairs)  28 us
    pallas_call x1, Pallas kernels, factorize(): pl.pallas_call(functools.partial(factor_kernel, scale=scale), in_specs=[S...  22.2 us
    all_to_all x1, blocking collectives, sum_devices(): lax.all_to_all(kept.reshape(plane, part, width), ('x', 'y'), 0, 0, tiled=...  19.2 us
    all_to_all x1, blocking collectives, sum_devices(): kept = lax.all_to_all(copies, ('x', 'y'), 0, 0, tiled=True).reshape(shape)  11.5 us
    all_to_all x1, blocking collectives, sum_devices(): piece = lax.all_to_all(copies, 'z', 0, 0, tiled=True).sum(0)  10.9 us
    ppermute x2, starting transfers between devices, local(): before = [lax.ppermute(part, TILE, up) for part in (first, second)]  7.1 us
    ppermute x2, waiting for transfers between devices, local(): after = [lax.ppermute(part, TILE, down) for part in (first, second)]  4.78 us
    ppermute x1, starting transfers between devices, sum_devices(): return (kept, lax.ppermute(kept, 'core', swap))  4.32 us
  transfers between devices with their start and end apart: 13, of which 6 were waited for; matrix products, arithmetic and copies ran while one was open for 0% of the time, Pallas kernels for 0%

profile of v2, /device:TPU:1, one launch (start us, length us, event | category | flops | bytes accessed | tf_op | source)
XLA Modules:
  0.0 128.5 jit_solution(10373985007172563533)
XLA Ops:
  0.6 1.8 %copy.8 = bf16[64,2,1,4096]{3,0,1,2:T(8,128)(2,1)S(1)} copy(bf16[64,2,1,4096]{3,1,2,0:T(2,128)(2,1)} %param.1) | data formatting | bytes 2097152 | tf_op args[0]
  2.5 0.1 pad_add_fusion.where_ref
  2.5 0.9 spread_kernel.1
  3.5 6.9 %collective-permute-start = (bf16[2,136,512]{2,1,0:T(8,128)(2,1)S(1)}, bf16[2,136,512]{2,1,0:T(8,128)(2,1)S(1)}, u32[]{:S(2)}, u32[]{:S(2)}) collective-permute-start(bf16[2,136,512]{2,1,0:T(8,128)(2,1)S(1)} %get-tuple-element.16), channel_id=1, source_target_pairs={{0,64},{1,193},{32,96},{33,225},{64,128},{65,1},{96,160},{97,33},{... | collective-permute-start | bytes 835592 | tf_op jit(solution)/shard_map/ppermute | solution.py:96
  10.4 0.7 collective-permute-start.1
  11.1 2.5 %collective-permute-start.2 = (bf16[136,512]{1,0:T(8,128)(2,1)S(1)}, bf16[136,512]{1,0:T(8,128)(2,1)S(1)}, u32[]{:S(2)}, u32[]{:S(2)}) collective-permute-start(bf16[136,512]{1,0:T(8,128)(2,1)S(1)} %get-tuple-element.18), channel_id=1, source_target_pairs={{0,96},{1,97},{32,128},{33,129},{64,160},{65,161},{96,192},{97,193... | collective-permute-start | bytes 417800 | tf_op jit(solution)/shard_map/ppermute | solution.py:96
  13.6 0.0 collective-permute-start.3
  13.6 4.3 %collective-permute-start.5 = (bf16[136,512]{1,0:T(8,128)(2,1)S(1)}, bf16[136,512]{1,0:T(8,128)(2,1)S(1)}, u32[]{:S(2)}, u32[]{:S(2)}) collective-permute-start(bf16[136,512]{1,0:T(8,128)(2,1)S(1)} %get-tuple-element.20), channel_id=1, source_target_pairs={{0,224},{1,225},{32,0},{33,1},{64,32},{65,33},{96,64},{97,65},{128... | collective-permute-start | bytes 417800 | tf_op jit(solution)/shard_map/ppermute | solution.py:96
  18.0 0.0 collective-permute-done.refs_1_
  18.0 7.5 %collective-permute-start.6 = (bf16[136,512]{1,0:T(8,128)(2,1)S(1)}, bf16[136,512]{1,0:T(8,128)(2,1)S(1)}, u32[]{:S(2)}, u32[]{:S(2)}) collective-permute-start(bf16[136,512]{1,0:T(8,128)(2,1)S(1)} %get-tuple-element.21), channel_id=1, source_target_pairs={{0,32},{1,33},{32,64},{33,65},{64,96},{65,97},{96,128},{97,129},{1... | collective-permute-start | bytes 417800 | tf_op jit(solution)/shard_map/ppermute | solution.py:96
  25.5 1.3 %collective-permute-done.1.refs_2_ = bf16[136,512]{1,0:T(8,128)(2,1)S(1)} collective-permute-done((bf16[136,512]{1,0:T(8,128)(2,1)S(1)}, bf16[136,512]{1,0:T(8,128)(2,1)S(1)}, u32[]{:S(2)}, u32[]{:S(2)}) %collective-permute-start.1) | collective-permute-done | bytes 139296 | tf_op jit(solution)/shard_map/ppermute | solution.py:96
  26.8 6.0 %collective-permute-start.4 = (bf16[136,512]{1,0:T(8,128)(2,1)S(1)}, bf16[136,512]{1,0:T(8,128)(2,1)S(1)}, u32[]{:S(2)}, u32[]{:S(2)}) collective-permute-start(bf16[136,512]{1,0:T(8,128)(2,1)S(1)} %slice_bitcast_fusion), channel_id=1, source_target_pairs={{0,64},{1,193},{32,96},{33,225},{64,128},{65,1},{96,160},{97,33},{... | collective-permute-start | bytes 417800 | tf_op jit(solution)/shard_map/ppermute | solution.py:96
  32.8 0.0 collective-permute-done.2.refs_3_
  32.9 2.1 %collective-permute-start.9 = (bf16[4,136,512]{2,1,0:T(8,128)(2,1)S(1)}, bf16[4,136,512]{2,1,0:T(8,128)(2,1)S(1)}, u32[]{:S(2)}, u32[]{:S(2)}) collective-permute-start(bf16[4,136,512]{2,1,0:T(8,128)(2,1)S(1)} %collect_kernel.2.refs_0_), channel_id=1, source_target_pairs={{1,0},{2,1},{3,2},{4,3},{5,4},{6,5},{7,6},{8,7},{9,8},{10,9},{11,1... | collective-permute-start | bytes 1671176 | tf_op jit(solution)/shard_map/ppermute | solution.py:361
  35.0 0.0 collective-permute-done.3.refs_0_
  35.0 3.5 %collective-permute-start.7 = (bf16[4,136,512]{2,1,0:T(8,128)(2,1)S(1)}, bf16[4,136,512]{2,1,0:T(8,128)(2,1)S(1)}, u32[]{:S(2)}, u32[]{:S(2)}) collective-permute-start(bf16[4,136,512]{2,1,0:T(8,128)(2,1)S(1)} %collect_kernel.2.refs_0_), channel_id=1, source_target_pairs={{0,1},{1,2},{2,3},{3,4},{4,5},{5,6},{6,7},{7,8},{8,9},{9,10},{10,1... | collective-permute-start | bytes 1671176 | tf_op jit(solution)/shard_map/ppermute | solution.py:360
  38.5 0.0 collective-permute-done.5.refs_2_
  38.5 0.0 collective-permute-done.6.refs_3_
  38.5 0.0 collective-permute-done.4.refs_1_
  38.5 1.9 %collective-permute-start.10 = (bf16[4,136,512]{2,1,0:T(8,128)(2,1)S(1)}, bf16[4,136,512]{2,1,0:T(8,128)(2,1)S(1)}, u32[]{:S(2)}, u32[]{:S(2)}) collective-permute-start(bf16[4,136,512]{2,1,0:T(8,128)(2,1)S(1)} %collect_kernel.3.refs_1_), channel_id=1, source_target_pairs={{1,0},{2,1},{3,2},{4,3},{5,4},{6,5},{7,6},{8,7},{9,8},{10,9},{11,1... | collective-permute-start | bytes 1671176 | tf_op jit(solution)/shard_map/ppermute | solution.py:361
  40.5 3.6 %collective-permute-start.8 = (bf16[4,136,512]{2,1,0:T(8,128)(2,1)S(1)}, bf16[4,136,512]{2,1,0:T(8,128)(2,1)S(1)}, u32[]{:S(2)}, u32[]{:S(2)}) collective-permute-start(bf16[4,136,512]{2,1,0:T(8,128)(2,1)S(1)} %collect_kernel.3.refs_1_), channel_id=1, source_target_pairs={{0,1},{1,2},{2,3},{3,4},{4,5},{5,6},{6,7},{7,8},{8,9},{9,10},{10,1... | collective-permute-start | bytes 1671176 | tf_op jit(solution)/shard_map/ppermute | solution.py:360
  44.1 0.0 collective-permute-done.9.refs_4_
  44.1 0.8 collective-permute-done.7.refs_2_
  44.9 4.8 %collective-permute-done.10.refs_5_ = bf16[4,136,512]{2,1,0:T(8,128)(2,1)S(1)} collective-permute-done((bf16[4,136,512]{2,1,0:T(8,128)(2,1)S(1)}, bf16[4,136,512]{2,1,0:T(8,128)(2,1)S(1)}, u32[]{:S(2)}, u32[]{:S(2)}) %collective-permute-start.10) | collective-permute-done | bytes 557088 | tf_op jit(solution)/shard_map/ppermute | solution.py:361
  49.7 1.2 collective-permute-done.8.refs_3_
  50.9 3.6 %gram_kernel.1 = (bf16[3,512,512]{2,1,0:T(8,128)(2,1)S(1)}, f32[5,128,128]{2,1,0:T(8,128)S(1)}, f32[5,128,128]{2,1,0:T(8,128)S(1)}) custom-call(s32[4]{0:T(128)S(1)} %pad_add_fusion.where_ref, bf16[4,136,512]{2,1,0:T(8,128)(2,1)S(1)} %collect_kernel.2.refs_0_, bf16[4,136,512]{2,1,0:T(8,128)(2,1)S(1)} %collect_kernel.3.refs_1_, ...), custom_call_target="tpu_custom_call" | custom-call | tf_op jit(solution)/shard_map/gram_kernel/pallas_call | solution.py:191
  54.5 0.1 collective-permute-start.11
  54.6 1.6 %collective-permute-done.11 = f32[5,128,128]{2,1,0:T(8,128)S(1)} collective-permute-done((f32[5,128,128]{2,1,0:T(8,128)S(1)}, f32[5,128,128]{2,1,0:T(8,128)S(1)}, u32[]{:S(2)}, u32[]{:S(2)}) %collective-permute-start.11) | collective-permute-done | bytes 327712 | tf_op jit(solution)/shard_map/ppermute | solution.py:338
  56.2 19.2 %all_to_all.15 = f32[16,40,128]{2,1,0:T(8,128)S(1)} all-to-all(f32[16,40,128]{2,1,0:T(8,128)S(1)} %bitcast.21), channel_id=1, replica_groups=mesh['z'=8,'x'=4,'y'=4,'core'=2] {'x','y'}, dimensions={0} | all-to-all | bytes 655360 | tf_op jit(solution)/shard_map/all_to_all | solution.py:341
  75.5 10.9 %all_to_all.16 = f32[8,40,128]{2,1,0:T(8,128)S(1)} all-to-all(f32[8,40,128]{2,1,0:T(8,128)S(1)} %broadcast_in_dim.6), channel_id=1, replica_groups=mesh['z'=8,'x'=4,'y'=4,'core'=2] {'z'}, dimensions={0} | all-to-all | bytes 327680 | tf_op jit(solution)/shard_map/all_to_all | solution.py:343
  86.5 11.5 %all_to_all.17 = f32[16,40,128]{2,1,0:T(8,128)S(1)} all-to-all(f32[16,40,128]{2,1,0:T(8,128)S(1)} %broadcast_in_dim.7), channel_id=1, replica_groups=mesh['z'=8,'x'=4,'y'=4,'core'=2] {'x','y'}, dimensions={0} | all-to-all | bytes 655360 | tf_op jit(solution)/shard_map/all_to_all | solution.py:345
  98.0 4.3 %collective-permute-start.12 = (f32[5,128,128]{2,1,0:T(8,128)S(1)}, f32[5,128,128]{2,1,0:T(8,128)S(1)}, u32[]{:S(2)}, u32[]{:S(2)}) collective-permute-start(f32[5,128,128]{2,1,0:T(8,128)S(1)} %bitcast.18), channel_id=1, source_target_pairs={{0,1},{1,0},{2,3},{3,2},{4,5},{5,4},{6,7},{7,6},{8,9},{9,8},{10,11... | collective-permute-start | bytes 983048 | tf_op jit(solution)/shard_map/ppermute | solution.py:346
  102.3 1.3 collective-permute-done.12.other_ref
  103.6 22.2 %factor_kernel.1 = (f32[512,512]{1,0:T(8,128)}, bf16[512,512]{1,0:T(8,128)(2,1)S(1)}, bf16[512,512]{1,0:T(8,128)(2,1)S(1)}) custom-call(s32[4]{0:T(128)S(1)} %pad_add_fusion.where_ref, f32[5,128,128]{2,1,0:T(8,128)S(1)} %bitcast.19, f32[5,128,128]{2,1,0:T(8,128)S(1)} %collective-permute-done.12.other_ref), custom_call_target="tpu_custom_call" | custom-call | tf_op jit(solution)/shard_map/factor_kernel/pallas_call | solution.py:300
  125.8 2.7 %basis_kernel.1 = bf16[3,512,512]{2,1,0:T(8,128)(2,1)} custom-call(bf16[512,512]{1,0:T(8,128)(2,1)S(1)} %get-tuple-element.24.hi_ref, bf16[512,512]{1,0:T(8,128)(2,1)S(1)} %get-tuple-element.25.lo_ref, bf16[3,512,512]{2,1,0:T(8,128)(2,1)S(1)} %get-tuple-element.26.snap_ref), custom_call_target="tpu_custom_call" | custom-call | tf_op jit(solution)/shard_map/basis_kernel/pallas_call | solution.py:324
  (8 shorter events, 0.2 us)
Async XLA Ops:
  3.5 14.5 %collective-permute-start = (bf16[2,136,512]{2,1,0:T(8,128)(2,1)S(1)}, bf16[2,136,512]{2,1,0:T(8,128)(2,1)S(1)}, u32[]{:S(2)}, u32[]{:S(2)}) collective-permute-start(bf16[2,136,512]{2,1,0:T(8,128)(2,1)S(1)} %get-tuple-element.16), channel_id=1, source_target_pairs={{0,64},{1,193},{32,96},{33,225},{64,128},{65,1},{96,160},{97,33},{... | collective-permute-start | bytes 835592 | tf_op jit(solution)/shard_map/ppermute | solution.py:96
  10.4 16.5 %collective-permute-start.1 = (bf16[136,512]{1,0:T(8,128)(2,1)S(1)}, bf16[136,512]{1,0:T(8,128)(2,1)S(1)}, u32[]{:S(2)}, u32[]{:S(2)}) collective-permute-start(bf16[136,512]{1,0:T(8,128)(2,1)S(1)} %get-tuple-element.17), channel_id=1, source_target_pairs={{0,160},{1,161},{32,192},{33,193},{64,224},{65,225},{96,0},{97,1},... | collective-permute-start | bytes 417800 | tf_op jit(solution)/shard_map/ppermute | solution.py:96
  11.1 21.8 %collective-permute-start.2 = (bf16[136,512]{1,0:T(8,128)(2,1)S(1)}, bf16[136,512]{1,0:T(8,128)(2,1)S(1)}, u32[]{:S(2)}, u32[]{:S(2)}) collective-permute-start(bf16[136,512]{1,0:T(8,128)(2,1)S(1)} %get-tuple-element.18), channel_id=1, source_target_pairs={{0,96},{1,97},{32,128},{33,129},{64,160},{65,161},{96,192},{97,193... | collective-permute-start | bytes 417800 | tf_op jit(solution)/shard_map/ppermute | solution.py:96
  13.6 21.4 %collective-permute-start.3 = (bf16[136,512]{1,0:T(8,128)(2,1)S(1)}, bf16[136,512]{1,0:T(8,128)(2,1)S(1)}, u32[]{:S(2)}, u32[]{:S(2)}) collective-permute-start(bf16[136,512]{1,0:T(8,128)(2,1)S(1)} %get-tuple-element.19), channel_id=1, source_target_pairs={{0,192},{1,65},{32,224},{33,97},{64,0},{65,129},{96,32},{97,161},{... | collective-permute-start | bytes 417800 | tf_op jit(solution)/shard_map/ppermute | solution.py:96
  13.6 24.8 %collective-permute-start.5 = (bf16[136,512]{1,0:T(8,128)(2,1)S(1)}, bf16[136,512]{1,0:T(8,128)(2,1)S(1)}, u32[]{:S(2)}, u32[]{:S(2)}) collective-permute-start(bf16[136,512]{1,0:T(8,128)(2,1)S(1)} %get-tuple-element.20), channel_id=1, source_target_pairs={{0,224},{1,225},{32,0},{33,1},{64,32},{65,33},{96,64},{97,65},{128... | collective-permute-start | bytes 417800 | tf_op jit(solution)/shard_map/ppermute | solution.py:96
  18.0 20.5 %collective-permute-start.6 = (bf16[136,512]{1,0:T(8,128)(2,1)S(1)}, bf16[136,512]{1,0:T(8,128)(2,1)S(1)}, u32[]{:S(2)}, u32[]{:S(2)}) collective-permute-start(bf16[136,512]{1,0:T(8,128)(2,1)S(1)} %get-tuple-element.21), channel_id=1, source_target_pairs={{0,32},{1,33},{32,64},{33,65},{64,96},{65,97},{96,128},{97,129},{1... | collective-permute-start | bytes 417800 | tf_op jit(solution)/shard_map/ppermute | solution.py:96
  26.8 11.6 %collective-permute-start.4 = (bf16[136,512]{1,0:T(8,128)(2,1)S(1)}, bf16[136,512]{1,0:T(8,128)(2,1)S(1)}, u32[]{:S(2)}, u32[]{:S(2)}) collective-permute-start(bf16[136,512]{1,0:T(8,128)(2,1)S(1)} %slice_bitcast_fusion), channel_id=1, source_target_pairs={{0,64},{1,193},{32,96},{33,225},{64,128},{65,1},{96,160},{97,33},{... | collective-permute-start | bytes 417800 | tf_op jit(solution)/shard_map/ppermute | solution.py:96
  32.9 11.2 %collective-permute-start.9 = (bf16[4,136,512]{2,1,0:T(8,128)(2,1)S(1)}, bf16[4,136,512]{2,1,0:T(8,128)(2,1)S(1)}, u32[]{:S(2)}, u32[]{:S(2)}) collective-permute-start(bf16[4,136,512]{2,1,0:T(8,128)(2,1)S(1)} %collect_kernel.2.refs_0_), channel_id=1, source_target_pairs={{1,0},{2,1},{3,2},{4,3},{5,4},{6,5},{7,6},{8,7},{9,8},{10,9},{11,1... | collective-permute-start | bytes 1671176 | tf_op jit(solution)/shard_map/ppermute | solution.py:361
  35.0 9.9 %collective-permute-start.7 = (bf16[4,136,512]{2,1,0:T(8,128)(2,1)S(1)}, bf16[4,136,512]{2,1,0:T(8,128)(2,1)S(1)}, u32[]{:S(2)}, u32[]{:S(2)}) collective-permute-start(bf16[4,136,512]{2,1,0:T(8,128)(2,1)S(1)} %collect_kernel.2.refs_0_), channel_id=1, source_target_pairs={{0,1},{1,2},{2,3},{3,4},{4,5},{5,6},{6,7},{7,8},{8,9},{9,10},{10,1... | collective-permute-start | bytes 1671176 | tf_op jit(solution)/shard_map/ppermute | solution.py:360
  38.5 11.2 %collective-permute-start.10 = (bf16[4,136,512]{2,1,0:T(8,128)(2,1)S(1)}, bf16[4,136,512]{2,1,0:T(8,128)(2,1)S(1)}, u32[]{:S(2)}, u32[]{:S(2)}) collective-permute-start(bf16[4,136,512]{2,1,0:T(8,128)(2,1)S(1)} %collect_kernel.3.refs_1_), channel_id=1, source_target_pairs={{1,0},{2,1},{3,2},{4,3},{5,4},{6,5},{7,6},{8,7},{9,8},{10,9},{11,1... | collective-permute-start | bytes 1671176 | tf_op jit(solution)/shard_map/ppermute | solution.py:361
  40.5 10.4 %collective-permute-start.8 = (bf16[4,136,512]{2,1,0:T(8,128)(2,1)S(1)}, bf16[4,136,512]{2,1,0:T(8,128)(2,1)S(1)}, u32[]{:S(2)}, u32[]{:S(2)}) collective-permute-start(bf16[4,136,512]{2,1,0:T(8,128)(2,1)S(1)} %collect_kernel.3.refs_1_), channel_id=1, source_target_pairs={{0,1},{1,2},{2,3},{3,4},{4,5},{5,6},{6,7},{7,8},{8,9},{9,10},{10,1... | collective-permute-start | bytes 1671176 | tf_op jit(solution)/shard_map/ppermute | solution.py:360
  54.5 1.7 %collective-permute-start.11 = (f32[5,128,128]{2,1,0:T(8,128)S(1)}, f32[5,128,128]{2,1,0:T(8,128)S(1)}, u32[]{:S(2)}, u32[]{:S(2)}) collective-permute-start(f32[5,128,128]{2,1,0:T(8,128)S(1)} %get-tuple-element.23), channel_id=1, source_target_pairs={{0,1},{1,0},{2,3},{3,2},{4,5},{5,4},{6,7},{7,6},{8,9},{9,8},{10,11... | collective-permute-start | bytes 983048 | tf_op jit(solution)/shard_map/ppermute | solution.py:338
  98.0 5.6 %collective-permute-start.12 = (f32[5,128,128]{2,1,0:T(8,128)S(1)}, f32[5,128,128]{2,1,0:T(8,128)S(1)}, u32[]{:S(2)}, u32[]{:S(2)}) collective-permute-start(f32[5,128,128]{2,1,0:T(8,128)S(1)} %bitcast.18), channel_id=1, source_target_pairs={{0,1},{1,0},{2,3},{3,2},{4,5},{5,4},{6,7},{7,6},{8,9},{9,8},{10,11... | collective-permute-start | bytes 983048 | tf_op jit(solution)/shard_map/ppermute | solution.py:346

commit v3 on v2

--- a/solution.py
+++ b/solution.py
@@ -10,6 +10,7 @@
 
 TILE = ("x", "y", "core")
 SUB = 8
+NEAR = 2
 BLOCK = 128
 LANES = 128
 HIGH = lax.Precision.HIGHEST
@@ -21,13 +22,13 @@
 
 
 def turns(sign):
-    return [0, 2 * sign, -3, 3, -2 * sign, 4, -1, 1]
+    return [0, 2 * sign, -2 * sign, -1, 1, -3, 3, 4]
 
 
 def spread_kernel(where_ref, planes_ref, *outs):
     place, core = where_ref[0], where_ref[3]
     own_ref, pair_ref = outs[0], outs[1]
-    singles = dict(zip((2, 3, 4, 6, 7), outs[2:]))
+    singles = dict(zip((2, 3, 4, 5, 6), outs[2:]))
     width = own_ref.shape[1]
     fields, frames, total = planes_ref.shape
     peers = total // width
@@ -37,7 +38,7 @@
     last = ((row == 0) & (lane == LANES - 1)).astype(BF16)
     first = ((row == 1) & (lane == 0)).astype(BF16)
     for slot, offset in enumerate(turns(1 - 2 * core)):
-        out_ref = own_ref if slot == 0 else pair_ref.at[0] if slot == 1 else pair_ref.at[1] if slot == 5 else singles[slot]
+        out_ref = own_ref if slot == 0 else pair_ref.at[0] if slot == 1 else pair_ref.at[1] if slot == 7 else singles[slot]
         start = lax.rem(place + offset + peers, peers) * width
         left = pl.multiple_of(jnp.maximum(start - LANES, 0), LANES)
         right = pl.multiple_of(jnp.minimum(start + width, total - LANES), LANES)
@@ -97,20 +98,20 @@
 
 
 def exchange(where, planes, peers):
-    own, pair, minus3, plus3, back2, minus1, plus1 = spread(where, planes, peers)
+    own, pair, back2, minus1, plus1, minus3, plus3 = spread(where, planes, peers)
     pair = shifted(pair, 2, -2, peers)
+    back2 = shifted(back2, -2, 2, peers)
+    minus1 = shifted(minus1, -1, -1, peers)
+    plus1 = shifted(plus1, 1, 1, peers)
+    first = collect(own, pair, back2, minus1, plus1)
     minus3 = shifted(minus3, -3, -3, peers)
     plus3 = shifted(plus3, 3, 3, peers)
-    first = collect(own, pair, minus3, plus3)
-    back2 = shifted(back2, -2, 2, peers)
     relayed = shifted(pair[1], 2, -2, peers)
-    minus1 = shifted(minus1, -1, -1, peers)
-    plus1 = shifted(plus1, 1, 1, peers)
-    second = collect(back2, relayed, minus1, plus1)
+    second = collect(minus3, plus3, relayed)
     return first, second
 
 
-NEXT = (0, 4, 2, 3, 1, 5, 6, 7)
+NEXT = (0, 2, 1, 3, 4, 5, 6, 7)
 
 
 def row_derivative(center, before, after, first, final):
@@ -138,8 +139,8 @@
 def gram_kernel(where_ref, *refs):
     parts, snap_ref, kept_ref, sent_ref, both_ref = refs[:6], *refs[6:]
     center, before, after = parts[0:2], parts[2:4], parts[4:6]
-    half_peers, _, width = center[0].shape
-    peers = 2 * half_peers
+    early, _, width = center[0].shape
+    peers = early + center[1].shape[0]
     total = snap_ref.shape[1]
     frames = total // peers
     rows = 2 * frames
@@ -148,10 +149,10 @@
     row = lax.broadcasted_iota(jnp.int32, (SUB, LANES), 0)
     turn = (((0,), (0,)), ((), ()))
     for slot, offset in enumerate(turns(1 - 2 * where_ref[3])):
-        here = center[slot // half_peers].at[slot % half_peers]
-        beside = NEXT[slot]
-        above = before[beside // half_peers].at[beside % half_peers]
-        below = after[beside // half_peers].at[beside % half_peers]
+        chunk, skip = (0, 0) if slot < early else (1, early)
+        here = center[chunk].at[slot - skip]
+        above = before[chunk].at[NEXT[slot] - skip]
+        below = after[chunk].at[NEXT[slot] - skip]
         edges = here[rows:, :rows]
         left = lax.dot_general(edges, (row == 0).astype(BF16), turn, preferred_element_type=F32)
         right = lax.dot_general(edges, (row == 1).astype(BF16), turn, preferred_element_type=F32)
@@ -199,23 +200,52 @@
     )(where, *parts)
 
 
-def eliminate_block(rows):
+def split(x):
+    top = x.astype(BF16).astype(F32)
+    rest = x - top
+    middle = rest.astype(BF16).astype(F32)
+    return top, middle, rest - middle
+
+
+LEFT = (0, 0, 1, 1, 0, 2)
+RIGHT = (0, 1, 0, 1, 2, 0)
+TURNED = (((0,), (0,)), ((), ()))
+PLAIN = (((1,), (0,)), ((), ()))
+
+
+def thin_product(left, right):
+    lefts, rights = split(left), split(right)
+    lefts = jnp.concatenate([lefts[p] for p in LEFT], 0).astype(BF16)
+    rights = jnp.concatenate([rights[p] for p in RIGHT], 0).astype(BF16)
+    return lax.dot_general(lefts, rights, TURNED, preferred_element_type=F32)
+
+
+def long_product(left, right, turned):
+    lefts = jnp.concatenate([left[p] for p in LEFT], 0 if turned else 1)
+    rights = jnp.concatenate([right[p] for p in RIGHT], 0)
+    return lax.dot_general(lefts, rights, TURNED if turned else PLAIN, preferred_element_type=F32)
+
+
+def eliminate_block(rows, fillers, spread_ref):
     tiles = len(rows)
     lane = lax.broadcasted_iota(jnp.int32, (SUB, BLOCK), 1)
     sub = lax.broadcasted_iota(jnp.int32, (SUB, BLOCK), 0)
     upper, inverse = [], []
     rows = list(rows)
     for step in range(tiles):
+        for _ in range(-(-len(fillers) // (tiles - step))):
+            fillers.pop(0)()
         base = step * SUB
         block = rows[step]
         a = {}
         for j in range(SUB):
-            column = jnp.broadcast_to(block[:, base + j:base + j + 1], (SUB, BLOCK))
+            spread_ref[step % 2, j * SUB:(j + 1) * SUB, :] = jnp.broadcast_to(block[:, base + j:base + j + 1], (SUB, BLOCK))
             for i in range(j, SUB):
-                a[i, j] = jnp.broadcast_to(column[i:i + 1, :], (SUB, BLOCK))
+                a[i, j] = spread_ref[step % 2, pl.ds(j * SUB + i, SUB, stride=0), :]
         inside = (lane >= base) & (lane < base + SUB)
         seeded = jnp.where(inside, (lane - base == sub).astype(F32), block)
-        v = [jnp.broadcast_to(seeded[i:i + 1, :], (SUB, BLOCK)) for i in range(SUB)]
+        spread_ref[step % 2, SUB * SUB:, :] = seeded
+        v = [spread_ref[step % 2, pl.ds(SUB * SUB + i, SUB, stride=0), :] for i in range(SUB)]
         unit = {}
         pivot, root = [], []
         for j in range(SUB):
@@ -240,7 +270,7 @@
             corner = jnp.where(sub == i, line * root[i], corner)
         upper.append(jnp.where(lane >= base + SUB, done, corner))
         inverse.append(jnp.where(lane < base + SUB, done, 0.0))
-        for q in range(step + 1, tiles):
+        for q in range(step + 1, min(step + 1 + NEAR, tiles)):
             old = rows[q]
             acc = jnp.where(inside, 0.0, old)
             left = [jnp.broadcast_to(old[:, base + j:base + j + 1], (SUB, BLOCK)) for j in range(SUB)]
@@ -249,6 +279,10 @@
                     left[m] = left[m] - left[j] * unit[m, j]
                 acc = acc - left[j] * z[j]
             rows[q] = acc
+        if step + 1 + NEAR < tiles:
+            update = thin_product(done, done)
+            for q in range(step + 1 + NEAR, tiles):
+                rows[q] = jnp.where(inside, 0.0, rows[q]) - update[q * SUB:(q + 1) * SUB, :]
     return upper, inverse
 
 
@@ -256,80 +290,111 @@
     return slice(k * BLOCK, (k + 1) * BLOCK)
 
 
-def factor_kernel(where_ref, kept_ref, other_ref, factor_ref, hi_ref, lo_ref, both_ref, m_ref, t_ref, *, scale):
-    n = m_ref.shape[0]
+def factor_kernel(where_ref, kept_ref, other_ref, snap_ref, factor_hbm, basis_hbm, gram_ref, carry_ref, part_ref, factor_ref, basis_ref, spread_ref, sems, *, scale):
+    n = factor_ref.shape[0]
     blocks = n // BLOCK
     core = where_ref[3]
-    both_ref[core] = kept_ref[...]
-    both_ref[1 - core] = other_ref[...]
-    pairs = upper_blocks(blocks)
-    half = len(pairs) // 2
-    for k in range(1, blocks):
-        m_ref[span(k), :k * BLOCK] = jnp.zeros((BLOCK, k * BLOCK), F32)
-    for index, (row, col) in enumerate(pairs):
-        m_ref[span(row), span(col)] = both_ref[index // half, index % half]
+    gram_ref[core] = kept_ref[...]
+    gram_ref[1 - core] = other_ref[...]
+    place = {pair: index for index, pair in enumerate(upper_blocks(blocks))}
+    half = len(place) // 2
+
+    def gram(i, m):
+        return gram_ref.at[place[i, m] // half, place[i, m] % half]
+
+    def carried(i, j):
+        return carry_ref.at[i * (i - 1) // 2 + j]
+
+    def parts(k, m):
+        return [part_ref[k, p, :, span(m)] for p in range(3)]
+
+    def keep(k, m, value):
+        for p, part in enumerate(split(value)):
+            part_ref[k, p, :, span(m)] = part.astype(BF16)
+
+    def upper_panel(k, m):
+        value = long_product(parts(k, k), split_block(gram(k, m)[...]), False)
+        factor_ref[span(k), span(m)] = value * (1.0 / scale)
+        keep(k, m, value)
+
+    def split_block(value):
+        return [part.astype(BF16) for part in split(value)]
+
+    def update_gram(k, i, m):
+        ref = gram(i, m)
+        ref[...] = ref[...] - long_product(parts(k, i), parts(k, m), True)
+
+    def update_carried(k, i, j):
+        ref = carried(i, j)
+        product = long_product(parts(k, i), parts(k, j), True)
+        ref[...] = -product if j == k else ref[...] - product
+
+    def lower_panel(k, j):
+        keep(k, j, long_product(parts(k, k), split_block(carried(k, j)[...]), False))
+
+    def basis_rows(k, c):
+        depth = (k + 1) * BLOCK
+        snap = snap_ref[c, :depth, :]
+        total = jnp.dot(part_ref[k, 0, :, :depth], snap, preferred_element_type=F32)
+        total = total + jnp.dot(part_ref[k, 1, :, :depth], snap, preferred_element_type=F32)
+        basis_ref[c, span(k), :] = (total * scale).astype(BF16)
+
+    def copies(k):
+        return (
+            pltpu.make_async_copy(basis_ref.at[:, span(k), :], basis_hbm.at[:, span(k), :], sems.at[0, k]),
+            pltpu.make_async_copy(factor_ref.at[span(k), :], factor_hbm.at[span(k), :], sems.at[1, k]),
+        )
+
+    def send(k):
+        for copy in copies(k):
+            copy.start()
+
+    fillers = []
     for k in range(blocks):
-        rows = [m_ref[k * BLOCK + s:k * BLOCK + s + SUB, span(k)] for s in range(0, BLOCK, SUB)]
-        upper, inverse = eliminate_block(rows)
-        for s in range(BLOCK // SUB):
-            t_ref[s * SUB:(s + 1) * SUB, :] = inverse[s]
-            factor_ref[k * BLOCK + s * SUB:k * BLOCK + (s + 1) * SUB, span(k)] = upper[s] * (1.0 / scale)
-        t = t_ref[...]
-        m_ref[span(k), :] = lax.dot_general(t, m_ref[span(k), :], (((1,), (0,)), ((), ())), precision=HIGH, preferred_element_type=F32)
-        m_ref[span(k), span(k)] = t
-        rest = n - (k + 1) * BLOCK
-        if rest:
-            panel = m_ref[span(k), :]
-            below = slice((k + 1) * BLOCK, n)
-            m_ref[below, span(k)] = jnp.zeros((rest, BLOCK), F32)
-            m_ref[below, :] = m_ref[below, :] - lax.dot_general(panel[:, (k + 1) * BLOCK:], panel, (((0,), (0,)), ((), ())), precision=HIGH, preferred_element_type=F32)
-    col = lax.broadcasted_iota(jnp.int32, (BLOCK, n), 1)
-    for k in range(blocks):
-        whole = m_ref[span(k), :]
-        if k + 1 < blocks:
-            factor_ref[span(k), (k + 1) * BLOCK:] = whole[:, (k + 1) * BLOCK:] * (1.0 / scale)
+        diagonal = gram(k, k)
+        rows = [diagonal[s:s + SUB, :] for s in range(0, BLOCK, SUB)]
+        upper, inverse = eliminate_block(rows, fillers, spread_ref)
+        keep(k, k, jnp.concatenate(inverse, 0))
+        factor_ref[span(k), span(k)] = jnp.concatenate(upper, 0) * (1.0 / scale)
         if k:
             factor_ref[span(k), :k * BLOCK] = jnp.zeros((BLOCK, k * BLOCK), F32)
-        inv = jnp.where(col < (k + 1) * BLOCK, whole, 0.0) * scale
-        hi = inv.astype(BF16)
-        hi_ref[span(k), :] = hi
-        lo_ref[span(k), :] = (inv - hi.astype(F32)).astype(BF16)
-
-
-def factorize(where, kept, other, n, scale):
+        later = range(k + 1, blocks)
+        if later:
+            upper_panel(k, k + 1)
+            update_gram(k, k + 1, k + 1)
+        fillers = [functools.partial(upper_panel, k, m) for m in later[1:]]
+        fillers += [functools.partial(lower_panel, k, j) for j in range(k)]
+        fillers += [functools.partial(update_gram, k, i, m) for i in later for m in range(i, blocks) if (i, m) != (k + 1, k + 1)]
+        fillers += [functools.partial(update_carried, k, i, j) for i in later for j in range(k + 1)]
+        fillers += [functools.partial(basis_rows, k, c) for c in range(snap_ref.shape[0])]
+        fillers.append(functools.partial(send, k))
+    for filler in fillers:
+        filler()
+    for k in range(blocks):
+        for copy in copies(k):
+            copy.wait()
+
+
+def factorize(where, kept, other, snap, scale):
+    n = snap.shape[1]
+    blocks = n // BLOCK
     return pl.pallas_call(
         functools.partial(factor_kernel, scale=scale),
-        in_specs=[SMEM, VMEM, VMEM],
-        out_specs=[VMEM] * 3,
-        out_shape=[jax.ShapeDtypeStruct((n, n), F32)] + [jax.ShapeDtypeStruct((n, n), BF16)] * 2,
-        scratch_shapes=[pltpu.VMEM((2,) + kept.shape, F32), pltpu.VMEM((n, n), F32), pltpu.VMEM((BLOCK, BLOCK), F32)],
+        in_specs=[SMEM, VMEM, VMEM, VMEM],
+        out_specs=[pl.BlockSpec(memory_space=pl.ANY)] * 2,
+        out_shape=[jax.ShapeDtypeStruct((n, n), F32), jax.ShapeDtypeStruct(snap.shape, BF16)],
+        scratch_shapes=[
+            pltpu.VMEM((2,) + kept.shape, F32),
+            pltpu.VMEM((blocks * (blocks - 1) // 2, BLOCK, BLOCK), F32),
+            pltpu.VMEM((blocks, 3, BLOCK, n), BF16),
+            pltpu.VMEM((n, n), F32),
+            pltpu.VMEM(snap.shape, BF16),
+            pltpu.VMEM((2, SUB * (SUB + 1), BLOCK), F32),
+            pltpu.SemaphoreType.DMA((2, blocks)),
+        ],
         compiler_params=PARAMS,
         name="factor_kernel",
-    )(where, kept, other)
-
-
-def basis_kernel(hi_ref, lo_ref, snap_ref, out_ref):
-    n = hi_ref.shape[0]
-    chunk = n // 2
-    for r in range(2):
-        rows, depth = slice(r * chunk, (r + 1) * chunk), (r + 1) * chunk
-        part = snap_ref[0, :depth, :]
-        total = jnp.dot(hi_ref[rows, :depth], part, preferred_element_type=F32)
-        total = total + jnp.dot(lo_ref[rows, :depth], part, preferred_element_type=F32)
-        out_ref[0, rows, :] = total.astype(BF16)
-
-
-def make_basis(hi, lo, snap):
-    block = pl.BlockSpec((1,) + snap.shape[1:], lambda c: (c, 0, 0))
-    return pl.pallas_call(
-        basis_kernel,
-        grid=(snap.shape[0],),
-        in_specs=[VMEM, VMEM, block],
-        out_specs=block,
-        out_shape=jax.ShapeDtypeStruct(snap.shape, BF16),
-        compiler_params=PARAMS,
-        name="basis_kernel",
-    )(hi, lo, snap)
+    )(where, kept, other, snap)
 
 
 def sum_devices(kept, sent):
@@ -361,8 +426,7 @@
     after = [lax.ppermute(part, TILE, down) for part in (first, second)]
     snap, kept, sent = cross_products(where, [first, second] + before + after, total_frames)
     kept, other = sum_devices(kept, sent)
-    factor, hi, lo = factorize(where, kept, other, total_frames, scale)
-    basis = make_basis(hi, lo, snap)
+    factor, basis = factorize(where, kept, other, snap, scale)
     return basis.transpose(1, 0, 2)[:, :, None, :], factor
 
 

time: 129 us -> 122 us (0.946)
  waiting for transfers between devices: 11 us -> 24 us
  starting transfers between devices: 43.5 us -> 31.5 us
  Pallas kernels: 29.5 us -> 21.2 us
    ppermute x7, waiting for transfers between devices: 1.35 us -> 16.1 us  [shifted(): return lax.ppermute(block, ('z', 'core'), pairs)]
    ppermute x7, starting transfers between devices: 28 us -> 16 us  [shifted(): return lax.ppermute(block, ('z', 'core'), pairs)]
    pallas_call x1, Pallas kernels: 22.2 us -> 16.6 us  [factorize(): pl.pallas_call(functools.partial(factor_kernel, scale=scale), in_specs=[S...]
    pallas_call x1 -> x0, Pallas kernels: 2.74 us -> none  [make_basis(): pl.pallas_call(basis_kernel, grid=(snap.shape[0],), in_specs=[VMEM, VMEM,...]
  transfers between devices with their start and end apart: 13 -> 13, of which waited for: 6 -> 7; matrix products, arithmetic and copies ran while one was open for 0% -> 0% of each run, Pallas kernels for 0% -> 0%
where the time goes in v3:
time: 122 us
  blocking collectives  42.2 us (35%)
  starting transfers between devices  31.5 us (26%)
  waiting for transfers between devices  24 us (20%)
  Pallas kernels  21.2 us (17%)
  local copies, waits for them, and re-layouts  1.85 us (2%)
    all_to_all x1, blocking collectives, sum_devices(): lax.all_to_all(kept.reshape(plane, part, width), ('x', 'y'), 0, 0, tiled=...  19.1 us
    pallas_call x1, Pallas kernels, factorize(): pl.pallas_call(functools.partial(factor_kernel, scale=scale), in_specs=[S...  16.6 us
    ppermute x7, waiting for transfers between devices, shifted(): return lax.ppermute(block, ('z', 'core'), pairs)  16.1 us
    ppermute x7, starting transfers between devices, shifted(): return lax.ppermute(block, ('z', 'core'), pairs)  16 us
    all_to_all x1, blocking collectives, sum_devices(): piece = lax.all_to_all(copies, 'z', 0, 0, tiled=True).sum(0)  11.6 us
    all_to_all x1, blocking collectives, sum_devices(): kept = lax.all_to_all(copies, ('x', 'y'), 0, 0, tiled=True).reshape(shape)  11.5 us
    ppermute x2, starting transfers between devices, local(): before = [lax.ppermute(part, TILE, up) for part in (first, second)]  7.16 us
    ppermute x1, starting transfers between devices, sum_devices(): return (kept, lax.ppermute(kept, 'core', swap))  4.32 us
  transfers between devices with their start and end apart: 13, of which 7 were waited for; matrix products, arithmetic and copies ran while one was open for 0% of the time, Pallas kernels for 0%

profile of v3, /device:TPU:1, one launch (start us, length us, event | category | flops | bytes accessed | tf_op | source)
XLA Modules:
  0.0 121.7 jit_solution(8921013352263979910)
XLA Ops:
  0.6 1.8 %copy.8 = bf16[64,2,1,4096]{3,0,1,2:T(8,128)(2,1)S(1)} copy(bf16[64,2,1,4096]{3,1,2,0:T(2,128)(2,1)} %param.1) | data formatting | bytes 2097152 | tf_op args[0]
  2.5 0.1 pad_add_fusion.where_ref
  2.5 0.9 spread_kernel.1
  3.5 6.9 %collective-permute-start = (bf16[2,136,512]{2,1,0:T(8,128)(2,1)S(1)}, bf16[2,136,512]{2,1,0:T(8,128)(2,1)S(1)}, u32[]{:S(2)}, u32[]{:S(2)}) collective-permute-start(bf16[2,136,512]{2,1,0:T(8,128)(2,1)S(1)} %get-tuple-element.15), channel_id=1, source_target_pairs={{0,64},{1,193},{32,96},{33,225},{64,128},{65,1},{96,160},{97,33},{... | collective-permute-start | bytes 835592 | tf_op jit(solution)/shard_map/ppermute | solution.py:97
  10.4 0.0 collective-permute-start.1
  10.4 3.1 %collective-permute-start.2 = (bf16[136,512]{1,0:T(8,128)(2,1)S(1)}, bf16[136,512]{1,0:T(8,128)(2,1)S(1)}, u32[]{:S(2)}, u32[]{:S(2)}) collective-permute-start(bf16[136,512]{1,0:T(8,128)(2,1)S(1)} %get-tuple-element.17), channel_id=1, source_target_pairs={{0,224},{1,225},{32,0},{33,1},{64,32},{65,33},{96,64},{97,65},{128... | collective-permute-start | bytes 417800 | tf_op jit(solution)/shard_map/ppermute | solution.py:97
  13.5 0.0 collective-permute-start.3
  13.5 1.6 %collective-permute-start.4 = (bf16[136,512]{1,0:T(8,128)(2,1)S(1)}, bf16[136,512]{1,0:T(8,128)(2,1)S(1)}, u32[]{:S(2)}, u32[]{:S(2)}) collective-permute-start(bf16[136,512]{1,0:T(8,128)(2,1)S(1)} %get-tuple-element.19), channel_id=1, source_target_pairs={{0,160},{1,161},{32,192},{33,193},{64,224},{65,225},{96,0},{97,1},... | collective-permute-start | bytes 417800 | tf_op jit(solution)/shard_map/ppermute | solution.py:97
  15.1 3.6 %collective-permute-done.1.refs_2_ = bf16[136,512]{1,0:T(8,128)(2,1)S(1)} collective-permute-done((bf16[136,512]{1,0:T(8,128)(2,1)S(1)}, bf16[136,512]{1,0:T(8,128)(2,1)S(1)}, u32[]{:S(2)}, u32[]{:S(2)}) %collective-permute-start.1) | collective-permute-done | bytes 139296 | tf_op jit(solution)/shard_map/ppermute | solution.py:97
  18.7 1.9 %collective-permute-start.5 = (bf16[136,512]{1,0:T(8,128)(2,1)S(1)}, bf16[136,512]{1,0:T(8,128)(2,1)S(1)}, u32[]{:S(2)}, u32[]{:S(2)}) collective-permute-start(bf16[136,512]{1,0:T(8,128)(2,1)S(1)} %get-tuple-element.20), channel_id=1, source_target_pairs={{0,96},{1,97},{32,128},{33,129},{64,160},{65,161},{96,192},{97,193... | collective-permute-start | bytes 417800 | tf_op jit(solution)/shard_map/ppermute | solution.py:97
  20.5 9.1 %collective-permute-done.2.refs_3_ = bf16[136,512]{1,0:T(8,128)(2,1)S(1)} collective-permute-done((bf16[136,512]{1,0:T(8,128)(2,1)S(1)}, bf16[136,512]{1,0:T(8,128)(2,1)S(1)}, u32[]{:S(2)}, u32[]{:S(2)}) %collective-permute-start.2) | collective-permute-done | bytes 139296 | tf_op jit(solution)/shard_map/ppermute | solution.py:97
  29.6 0.0 collective-permute-done.3.refs_4_
  29.6 0.0 collective-permute-done.refs_1_
  29.7 1.9 %collective-permute-start.9 = (bf16[5,136,512]{2,1,0:T(8,128)(2,1)S(1)}, bf16[5,136,512]{2,1,0:T(8,128)(2,1)S(1)}, u32[]{:S(2)}, u32[]{:S(2)}) collective-permute-start(bf16[5,136,512]{2,1,0:T(8,128)(2,1)S(1)} %collect_kernel.2.refs_0_), channel_id=1, source_target_pairs={{1,0},{2,1},{3,2},{4,3},{5,4},{6,5},{7,6},{8,7},{9,8},{10,9},{11,1... | collective-permute-start | bytes 2088968 | tf_op jit(solution)/shard_map/ppermute | solution.py:426
  31.6 3.6 %collective-permute-start.7 = (bf16[5,136,512]{2,1,0:T(8,128)(2,1)S(1)}, bf16[5,136,512]{2,1,0:T(8,128)(2,1)S(1)}, u32[]{:S(2)}, u32[]{:S(2)}) collective-permute-start(bf16[5,136,512]{2,1,0:T(8,128)(2,1)S(1)} %collect_kernel.2.refs_0_), channel_id=1, source_target_pairs={{0,1},{1,2},{2,3},{3,4},{4,5},{5,6},{6,7},{7,8},{8,9},{9,10},{10,1... | collective-permute-start | bytes 2088968 | tf_op jit(solution)/shard_map/ppermute | solution.py:425
  35.3 2.5 %collective-permute-start.6 = (bf16[136,512]{1,0:T(8,128)(2,1)S(1)}, bf16[136,512]{1,0:T(8,128)(2,1)S(1)}, u32[]{:S(2)}, u32[]{:S(2)}) collective-permute-start(bf16[136,512]{1,0:T(8,128)(2,1)S(1)} %slice_bitcast_fusion), channel_id=1, source_target_pairs={{0,64},{1,193},{32,96},{33,225},{64,128},{65,1},{96,160},{97,33},{... | collective-permute-start | bytes 417800 | tf_op jit(solution)/shard_map/ppermute | solution.py:97
  37.8 0.0 collective-permute-done.4.refs_0_
  37.8 0.0 collective-permute-done.5.refs_1_
  37.8 3.5 %collective-permute-done.6.refs_2_ = bf16[136,512]{1,0:T(8,128)(2,1)S(1)} collective-permute-done((bf16[136,512]{1,0:T(8,128)(2,1)S(1)}, bf16[136,512]{1,0:T(8,128)(2,1)S(1)}, u32[]{:S(2)}, u32[]{:S(2)}) %collective-permute-start.6) | collective-permute-done | bytes 139296 | tf_op jit(solution)/shard_map/ppermute | solution.py:97
  41.2 2.0 %collective-permute-start.10 = (bf16[3,136,512]{2,1,0:T(8,128)(2,1)S(1)}, bf16[3,136,512]{2,1,0:T(8,128)(2,1)S(1)}, u32[]{:S(2)}, u32[]{:S(2)}) collective-permute-start(bf16[3,136,512]{2,1,0:T(8,128)(2,1)S(1)} %collect_kernel.3.refs_1_), channel_id=1, source_target_pairs={{1,0},{2,1},{3,2},{4,3},{5,4},{6,5},{7,6},{8,7},{9,8},{10,9},{11,1... | collective-permute-start | bytes 1253384 | tf_op jit(solution)/shard_map/ppermute | solution.py:426
  43.3 3.5 %collective-permute-start.8 = (bf16[3,136,512]{2,1,0:T(8,128)(2,1)S(1)}, bf16[3,136,512]{2,1,0:T(8,128)(2,1)S(1)}, u32[]{:S(2)}, u32[]{:S(2)}) collective-permute-start(bf16[3,136,512]{2,1,0:T(8,128)(2,1)S(1)} %collect_kernel.3.refs_1_), channel_id=1, source_target_pairs={{0,1},{1,2},{2,3},{3,4},{4,5},{5,6},{6,7},{7,8},{8,9},{9,10},{10,1... | collective-permute-start | bytes 1253384 | tf_op jit(solution)/shard_map/ppermute | solution.py:425
  46.8 3.8 %collective-permute-done.10.refs_5_ = bf16[3,136,512]{2,1,0:T(8,128)(2,1)S(1)} collective-permute-done((bf16[3,136,512]{2,1,0:T(8,128)(2,1)S(1)}, bf16[3,136,512]{2,1,0:T(8,128)(2,1)S(1)}, u32[]{:S(2)}, u32[]{:S(2)}) %collective-permute-start.10) | collective-permute-done | bytes 417824 | tf_op jit(solution)/shard_map/ppermute | solution.py:426
  50.6 1.2 collective-permute-done.8.refs_3_
  51.8 0.0 collective-permute-done.9.refs_4_
  51.8 0.0 collective-permute-done.7.refs_2_
  51.8 3.6 %gram_kernel.1 = (bf16[3,512,512]{2,1,0:T(8,128)(2,1)S(1)}, f32[5,128,128]{2,1,0:T(8,128)S(1)}, f32[5,128,128]{2,1,0:T(8,128)S(1)}) custom-call(s32[4]{0:T(128)S(1)} %pad_add_fusion.where_ref, bf16[5,136,512]{2,1,0:T(8,128)(2,1)S(1)} %collect_kernel.2.refs_0_, bf16[3,136,512]{2,1,0:T(8,128)(2,1)S(1)} %collect_kernel.3.refs_1_, ...), custom_call_target="tpu_custom_call" | custom-call | tf_op jit(solution)/shard_map/gram_kernel/pallas_call | solution.py:192
  55.4 0.1 collective-permute-start.11
  55.5 1.6 %collective-permute-done.11 = f32[5,128,128]{2,1,0:T(8,128)S(1)} collective-permute-done((f32[5,128,128]{2,1,0:T(8,128)S(1)}, f32[5,128,128]{2,1,0:T(8,128)S(1)}, u32[]{:S(2)}, u32[]{:S(2)}) %collective-permute-start.11) | collective-permute-done | bytes 327712 | tf_op jit(solution)/shard_map/ppermute | solution.py:403
  57.1 19.1 %all_to_all.15 = f32[16,40,128]{2,1,0:T(8,128)S(1)} all-to-all(f32[16,40,128]{2,1,0:T(8,128)S(1)} %bitcast.20), channel_id=1, replica_groups=mesh['z'=8,'x'=4,'y'=4,'core'=2] {'x','y'}, dimensions={0} | all-to-all | bytes 655360 | tf_op jit(solution)/shard_map/all_to_all | solution.py:406
  76.3 11.6 %all_to_all.16 = f32[8,40,128]{2,1,0:T(8,128)S(1)} all-to-all(f32[8,40,128]{2,1,0:T(8,128)S(1)} %broadcast_in_dim.6), channel_id=1, replica_groups=mesh['z'=8,'x'=4,'y'=4,'core'=2] {'z'}, dimensions={0} | all-to-all | bytes 327680 | tf_op jit(solution)/shard_map/all_to_all | solution.py:408
  87.9 11.5 %all_to_all.17 = f32[16,40,128]{2,1,0:T(8,128)S(1)} all-to-all(f32[16,40,128]{2,1,0:T(8,128)S(1)} %broadcast_in_dim.7), channel_id=1, replica_groups=mesh['z'=8,'x'=4,'y'=4,'core'=2] {'x','y'}, dimensions={0} | all-to-all | bytes 655360 | tf_op jit(solution)/shard_map/all_to_all | solution.py:410
  99.4 4.3 %collective-permute-start.12 = (f32[5,128,128]{2,1,0:T(8,128)S(1)}, f32[5,128,128]{2,1,0:T(8,128)S(1)}, u32[]{:S(2)}, u32[]{:S(2)}) collective-permute-start(f32[5,128,128]{2,1,0:T(8,128)S(1)} %bitcast.18), channel_id=1, source_target_pairs={{0,1},{1,0},{2,3},{3,2},{4,5},{5,4},{6,7},{7,6},{8,9},{9,8},{10,11... | collective-permute-start | bytes 983048 | tf_op jit(solution)/shard_map/ppermute | solution.py:411
  103.7 1.3 %collective-permute-done.12.other_ref = f32[5,128,128]{2,1,0:T(8,128)S(1)} collective-permute-done((f32[5,128,128]{2,1,0:T(8,128)S(1)}, f32[5,128,128]{2,1,0:T(8,128)S(1)}, u32[]{:S(2)}, u32[]{:S(2)}) %collective-permute-start.12) | collective-permute-done | bytes 327712 | tf_op jit(solution)/shard_map/ppermute | solution.py:411
  105.0 16.6 %factor_kernel.1 = (f32[512,512]{1,0:T(8,128)}, bf16[3,512,512]{2,1,0:T(8,128)(2,1)}) custom-call(s32[4]{0:T(128)S(1)} %pad_add_fusion.where_ref, f32[5,128,128]{2,1,0:T(8,128)S(1)} %bitcast.19, f32[5,128,128]{2,1,0:T(8,128)S(1)} %collective-permute-done.12.other_ref, bf16[3,512,512]{2,1,0:T(8,128)(2,1)S(1)} %get-tuple-element.23.snap_ref), custom_call_target="tpu_custom_call" | custom-call | tf_op jit(solution)/shard_map/factor_kernel/pallas_call | solution.py:381
  (8 shorter events, 0.2 us)
Async XLA Ops:
  3.5 26.2 %collective-permute-start = (bf16[2,136,512]{2,1,0:T(8,128)(2,1)S(1)}, bf16[2,136,512]{2,1,0:T(8,128)(2,1)S(1)}, u32[]{:S(2)}, u32[]{:S(2)}) collective-permute-start(bf16[2,136,512]{2,1,0:T(8,128)(2,1)S(1)} %get-tuple-element.15), channel_id=1, source_target_pairs={{0,64},{1,193},{32,96},{33,225},{64,128},{65,1},{96,160},{97,33},{... | collective-permute-start | bytes 835592 | tf_op jit(solution)/shard_map/ppermute | solution.py:97
  10.4 8.3 %collective-permute-start.1 = (bf16[136,512]{1,0:T(8,128)(2,1)S(1)}, bf16[136,512]{1,0:T(8,128)(2,1)S(1)}, u32[]{:S(2)}, u32[]{:S(2)}) collective-permute-start(bf16[136,512]{1,0:T(8,128)(2,1)S(1)} %get-tuple-element.16), channel_id=1, source_target_pairs={{0,192},{1,65},{32,224},{33,97},{64,0},{65,129},{96,32},{97,161},{... | collective-permute-start | bytes 417800 | tf_op jit(solution)/shard_map/ppermute | solution.py:97
  10.4 19.3 %collective-permute-start.2 = (bf16[136,512]{1,0:T(8,128)(2,1)S(1)}, bf16[136,512]{1,0:T(8,128)(2,1)S(1)}, u32[]{:S(2)}, u32[]{:S(2)}) collective-permute-start(bf16[136,512]{1,0:T(8,128)(2,1)S(1)} %get-tuple-element.17), channel_id=1, source_target_pairs={{0,224},{1,225},{32,0},{33,1},{64,32},{65,33},{96,64},{97,65},{128... | collective-permute-start | bytes 417800 | tf_op jit(solution)/shard_map/ppermute | solution.py:97
  13.5 16.1 %collective-permute-start.3 = (bf16[136,512]{1,0:T(8,128)(2,1)S(1)}, bf16[136,512]{1,0:T(8,128)(2,1)S(1)}, u32[]{:S(2)}, u32[]{:S(2)}) collective-permute-start(bf16[136,512]{1,0:T(8,128)(2,1)S(1)} %get-tuple-element.18), channel_id=1, source_target_pairs={{0,32},{1,33},{32,64},{33,65},{64,96},{65,97},{96,128},{97,129},{1... | collective-permute-start | bytes 417800 | tf_op jit(solution)/shard_map/ppermute | solution.py:97
  13.5 24.3 %collective-permute-start.4 = (bf16[136,512]{1,0:T(8,128)(2,1)S(1)}, bf16[136,512]{1,0:T(8,128)(2,1)S(1)}, u32[]{:S(2)}, u32[]{:S(2)}) collective-permute-start(bf16[136,512]{1,0:T(8,128)(2,1)S(1)} %get-tuple-element.19), channel_id=1, source_target_pairs={{0,160},{1,161},{32,192},{33,193},{64,224},{65,225},{96,0},{97,1},... | collective-permute-start | bytes 417800 | tf_op jit(solution)/shard_map/ppermute | solution.py:97
  18.7 19.1 %collective-permute-start.5 = (bf16[136,512]{1,0:T(8,128)(2,1)S(1)}, bf16[136,512]{1,0:T(8,128)(2,1)S(1)}, u32[]{:S(2)}, u32[]{:S(2)}) collective-permute-start(bf16[136,512]{1,0:T(8,128)(2,1)S(1)} %get-tuple-element.20), channel_id=1, source_target_pairs={{0,96},{1,97},{32,128},{33,129},{64,160},{65,161},{96,192},{97,193... | collective-permute-start | bytes 417800 | tf_op jit(solution)/shard_map/ppermute | solution.py:97
  29.7 22.1 %collective-permute-start.9 = (bf16[5,136,512]{2,1,0:T(8,128)(2,1)S(1)}, bf16[5,136,512]{2,1,0:T(8,128)(2,1)S(1)}, u32[]{:S(2)}, u32[]{:S(2)}) collective-permute-start(bf16[5,136,512]{2,1,0:T(8,128)(2,1)S(1)} %collect_kernel.2.refs_0_), channel_id=1, source_target_pairs={{1,0},{2,1},{3,2},{4,3},{5,4},{6,5},{7,6},{8,7},{9,8},{10,9},{11,1... | collective-permute-start | bytes 2088968 | tf_op jit(solution)/shard_map/ppermute | solution.py:426
  31.6 20.2 %collective-permute-start.7 = (bf16[5,136,512]{2,1,0:T(8,128)(2,1)S(1)}, bf16[5,136,512]{2,1,0:T(8,128)(2,1)S(1)}, u32[]{:S(2)}, u32[]{:S(2)}) collective-permute-start(bf16[5,136,512]{2,1,0:T(8,128)(2,1)S(1)} %collect_kernel.2.refs_0_), channel_id=1, source_target_pairs={{0,1},{1,2},{2,3},{3,4},{4,5},{5,6},{6,7},{7,8},{8,9},{9,10},{10,1... | collective-permute-start | bytes 2088968 | tf_op jit(solution)/shard_map/ppermute | solution.py:425
  35.3 5.9 %collective-permute-start.6 = (bf16[136,512]{1,0:T(8,128)(2,1)S(1)}, bf16[136,512]{1,0:T(8,128)(2,1)S(1)}, u32[]{:S(2)}, u32[]{:S(2)}) collective-permute-start(bf16[136,512]{1,0:T(8,128)(2,1)S(1)} %slice_bitcast_fusion), channel_id=1, source_target_pairs={{0,64},{1,193},{32,96},{33,225},{64,128},{65,1},{96,160},{97,33},{... | collective-permute-start | bytes 417800 | tf_op jit(solution)/shard_map/ppermute | solution.py:97
  41.2 9.4 %collective-permute-start.10 = (bf16[3,136,512]{2,1,0:T(8,128)(2,1)S(1)}, bf16[3,136,512]{2,1,0:T(8,128)(2,1)S(1)}, u32[]{:S(2)}, u32[]{:S(2)}) collective-permute-start(bf16[3,136,512]{2,1,0:T(8,128)(2,1)S(1)} %collect_kernel.3.refs_1_), channel_id=1, source_target_pairs={{1,0},{2,1},{3,2},{4,3},{5,4},{6,5},{7,6},{8,7},{9,8},{10,9},{11,1... | collective-permute-start | bytes 1253384 | tf_op jit(solution)/shard_map/ppermute | solution.py:426
  43.3 8.5 %collective-permute-start.8 = (bf16[3,136,512]{2,1,0:T(8,128)(2,1)S(1)}, bf16[3,136,512]{2,1,0:T(8,128)(2,1)S(1)}, u32[]{:S(2)}, u32[]{:S(2)}) collective-permute-start(bf16[3,136,512]{2,1,0:T(8,128)(2,1)S(1)} %collect_kernel.3.refs_1_), channel_id=1, source_target_pairs={{0,1},{1,2},{2,3},{3,4},{4,5},{5,6},{6,7},{7,8},{8,9},{9,10},{10,1... | collective-permute-start | bytes 1253384 | tf_op jit(solution)/shard_map/ppermute | solution.py:425
  55.4 1.7 %collective-permute-start.11 = (f32[5,128,128]{2,1,0:T(8,128)S(1)}, f32[5,128,128]{2,1,0:T(8,128)S(1)}, u32[]{:S(2)}, u32[]{:S(2)}) collective-permute-start(f32[5,128,128]{2,1,0:T(8,128)S(1)} %get-tuple-element.22), channel_id=1, source_target_pairs={{0,1},{1,0},{2,3},{3,2},{4,5},{5,4},{6,7},{7,6},{8,9},{9,8},{10,11... | collective-permute-start | bytes 983048 | tf_op jit(solution)/shard_map/ppermute | solution.py:403
  99.4 5.6 %collective-permute-start.12 = (f32[5,128,128]{2,1,0:T(8,128)S(1)}, f32[5,128,128]{2,1,0:T(8,128)S(1)}, u32[]{:S(2)}, u32[]{:S(2)}) collective-permute-start(f32[5,128,128]{2,1,0:T(8,128)S(1)} %bitcast.18), channel_id=1, source_target_pairs={{0,1},{1,0},{2,3},{3,2},{4,5},{5,4},{6,7},{7,6},{8,9},{9,8},{10,11... | collective-permute-start | bytes 983048 | tf_op jit(solution)/shard_map/ppermute | solution.py:411

commit v4 on v3

--- a/solution.py
+++ b/solution.py
@@ -114,10 +114,8 @@
 NEXT = (0, 2, 1, 3, 4, 5, 6, 7)
 
 
-def row_derivative(center, before, after, first, final):
-    after = jnp.where(final, center, after)
-    before = jnp.where(first, center, before)
-    return (after - before) * jnp.where(first | final, 1.0, 0.5)
+def row_derivative(center, inner, outer, edge, factor):
+    return (inner - jnp.where(edge, center, outer)) * factor
 
 
 def column_derivative(center, left, right, start, total):
@@ -138,28 +136,29 @@
 
 def gram_kernel(where_ref, *refs):
     parts, snap_ref, kept_ref, sent_ref, both_ref = refs[:6], *refs[6:]
-    center, before, after = parts[0:2], parts[2:4], parts[4:6]
+    center, inner, outer = parts[0:2], parts[2:4], parts[4:6]
     early, _, width = center[0].shape
     peers = early + center[1].shape[0]
     total = snap_ref.shape[1]
     frames = total // peers
     rows = 2 * frames
-    top, bottom = where_ref[1] == 0, where_ref[1] == where_ref[2] - 1
+    edge = (where_ref[1] == 0) | (where_ref[1] == where_ref[2] - 1)
+    factor = jnp.where(edge, 1.0, 0.5) * jnp.where(where_ref[3] == 0, 1.0, -1.0)
     start = where_ref[0] * width
     row = lax.broadcasted_iota(jnp.int32, (SUB, LANES), 0)
     turn = (((0,), (0,)), ((), ()))
     for slot, offset in enumerate(turns(1 - 2 * where_ref[3])):
         chunk, skip = (0, 0) if slot < early else (1, early)
         here = center[chunk].at[slot - skip]
-        above = before[chunk].at[NEXT[slot] - skip]
-        below = after[chunk].at[NEXT[slot] - skip]
+        near = inner[chunk].at[NEXT[slot] - skip]
+        far = outer[chunk].at[NEXT[slot] - skip]
         edges = here[rows:, :rows]
         left = lax.dot_general(edges, (row == 0).astype(BF16), turn, preferred_element_type=F32)
         right = lax.dot_general(edges, (row == 1).astype(BF16), turn, preferred_element_type=F32)
         u_rows, v_rows = slice(0, frames), slice(frames, rows)
         u, v = here[u_rows, :].astype(F32), here[v_rows, :].astype(F32)
-        slope_u = row_derivative(u, above[u_rows, :].astype(F32), below[u_rows, :].astype(F32), top, bottom)
-        slope_v = row_derivative(v, above[v_rows, :].astype(F32), below[v_rows, :].astype(F32), top, bottom)
+        slope_u = row_derivative(u, near[u_rows, :].astype(F32), far[u_rows, :].astype(F32), edge, factor)
+        slope_v = row_derivative(v, near[v_rows, :].astype(F32), far[v_rows, :].astype(F32), edge, factor)
         along_u = column_derivative(u, left[u_rows, :1], right[u_rows, :1], start, width * peers)
         along_v = column_derivative(v, left[v_rows, :1], right[v_rows, :1], start, width * peers)
         source = lax.rem(where_ref[0] + peers - offset, peers)
@@ -420,11 +419,11 @@
     where = jnp.stack([lax.axis_index("z"), lax.axis_index(TILE), jnp.int32(total_rows), lax.axis_index("core")]).astype(jnp.int32)
     planes = displacement.reshape(frames, 2, width).transpose(1, 0, 2)
     first, second = exchange(where, planes, peers)
-    up = [(i, i + 1) for i in range(total_rows - 1)]
-    down = [(j, i) for i, j in up]
-    before = [lax.ppermute(part, TILE, up) for part in (first, second)]
-    after = [lax.ppermute(part, TILE, down) for part in (first, second)]
-    snap, kept, sent = cross_products(where, [first, second] + before + after, total_frames)
+    chip = [(i, i ^ 1) for i in range(total_rows)]
+    between = [(i, ((i + 1) ^ 1) - 1) for i in range(1, total_rows - 1)]
+    inner = [lax.ppermute(part, TILE, chip) for part in (first, second)]
+    outer = [lax.ppermute(part, TILE, between) for part in (first, second)]
+    snap, kept, sent = cross_products(where, [first, second] + inner + outer, total_frames)
     kept, other = sum_devices(kept, sent)
     factor, basis = factorize(where, kept, other, snap, scale)
     return basis.transpose(1, 0, 2)[:, :, None, :], factor

time: 122 us -> 116 us (0.951)
  blocking collectives: 42.2 us -> 39.7 us
  starting transfers between devices: 31.5 us -> 29 us
    ppermute x4, starting transfers between devices: 11.1 us -> 6.93 us  [the longest x2 6.75 us: local(): outer = [lax.ppermute(part, TILE, between) for part in (first, second)]]
    all_to_all x1, blocking collectives: 19.1 us -> 16.3 us  [sum_devices(): lax.all_to_all(kept.reshape(plane, part, width), ('x', 'y'), 0, 0, tiled=...]
    ppermute x7, starting transfers between devices: 16 us -> 17.7 us  [shifted(): return lax.ppermute(block, ('z', 'core'), pairs)]
  transfers between devices with their start and end apart: 13 -> 13, of which waited for: 7 -> 6; matrix products, arithmetic and copies ran while one was open for 0% -> 0% of each run, Pallas kernels for 0% -> 0%
where the time goes in v4:
time: 116 us
  blocking collectives  39.7 us (34%)
  starting transfers between devices  29 us (25%)
  waiting for transfers between devices  23.4 us (20%)
  Pallas kernels  21.1 us (18%)
  local copies, waits for them, and re-layouts  1.85 us (2%)
    ppermute x7, starting transfers between devices, shifted(): return lax.ppermute(block, ('z', 'core'), pairs)  17.7 us
    pallas_call x1, Pallas kernels, factorize(): pl.pallas_call(functools.partial(factor_kernel, scale=scale), in_specs=[S...  16.6 us
    all_to_all x1, blocking collectives, sum_devices(): lax.all_to_all(kept.reshape(plane, part, width), ('x', 'y'), 0, 0, tiled=...  16.3 us
    ppermute x7, waiting for transfers between devices, shifted(): return lax.ppermute(block, ('z', 'core'), pairs)  15 us
    all_to_all x1, blocking collectives, sum_devices(): piece = lax.all_to_all(copies, 'z', 0, 0, tiled=True).sum(0)  11.9 us
    all_to_all x1, blocking collectives, sum_devices(): kept = lax.all_to_all(copies, ('x', 'y'), 0, 0, tiled=True).reshape(shape)  11.5 us
    ppermute x2, starting transfers between devices, local(): outer = [lax.ppermute(part, TILE, between) for part in (first, second)]  6.75 us
    ppermute x2, waiting for transfers between devices, local(): outer = [lax.ppermute(part, TILE, between) for part in (first, second)]  5.61 us
  transfers between devices with their start and end apart: 13, of which 6 were waited for; matrix products, arithmetic and copies ran while one was open for 0% of the time, Pallas kernels for 0%

profile of v4, /device:TPU:1, one launch (start us, length us, event | category | flops | bytes accessed | tf_op | source)
XLA Modules:
  0.0 116.2 jit_solution(4129390243937138178)
XLA Ops:
  0.6 1.8 %copy.8 = bf16[64,2,1,4096]{3,0,1,2:T(8,128)(2,1)S(1)} copy(bf16[64,2,1,4096]{3,1,2,0:T(2,128)(2,1)} %param.1) | data formatting | bytes 2097152 | tf_op args[0]
  2.5 0.1 pad_add_fusion.where_ref
  2.5 0.9 spread_kernel.1
  3.5 6.9 %collective-permute-start = (bf16[2,136,512]{2,1,0:T(8,128)(2,1)S(1)}, bf16[2,136,512]{2,1,0:T(8,128)(2,1)S(1)}, u32[]{:S(2)}, u32[]{:S(2)}) collective-permute-start(bf16[2,136,512]{2,1,0:T(8,128)(2,1)S(1)} %get-tuple-element.15), channel_id=1, source_target_pairs={{0,64},{1,193},{32,96},{33,225},{64,128},{65,1},{96,160},{97,33},{... | collective-permute-start | bytes 835592 | tf_op jit(solution)/shard_map/ppermute | solution.py:97
  10.4 0.0 collective-permute-start.1
  10.4 3.1 %collective-permute-start.2 = (bf16[136,512]{1,0:T(8,128)(2,1)S(1)}, bf16[136,512]{1,0:T(8,128)(2,1)S(1)}, u32[]{:S(2)}, u32[]{:S(2)}) collective-permute-start(bf16[136,512]{1,0:T(8,128)(2,1)S(1)} %get-tuple-element.17), channel_id=1, source_target_pairs={{0,224},{1,225},{32,0},{33,1},{64,32},{65,33},{96,64},{97,65},{128... | collective-permute-start | bytes 417800 | tf_op jit(solution)/shard_map/ppermute | solution.py:97
  13.5 0.0 collective-permute-start.3
  13.5 1.6 %collective-permute-start.4 = (bf16[136,512]{1,0:T(8,128)(2,1)S(1)}, bf16[136,512]{1,0:T(8,128)(2,1)S(1)}, u32[]{:S(2)}, u32[]{:S(2)}) collective-permute-start(bf16[136,512]{1,0:T(8,128)(2,1)S(1)} %get-tuple-element.19), channel_id=1, source_target_pairs={{0,160},{1,161},{32,192},{33,193},{64,224},{65,225},{96,0},{97,1},... | collective-permute-start | bytes 417800 | tf_op jit(solution)/shard_map/ppermute | solution.py:97
  15.1 3.6 %collective-permute-done.1.refs_2_ = bf16[136,512]{1,0:T(8,128)(2,1)S(1)} collective-permute-done((bf16[136,512]{1,0:T(8,128)(2,1)S(1)}, bf16[136,512]{1,0:T(8,128)(2,1)S(1)}, u32[]{:S(2)}, u32[]{:S(2)}) %collective-permute-start.1) | collective-permute-done | bytes 139296 | tf_op jit(solution)/shard_map/ppermute | solution.py:97
  18.7 1.9 %collective-permute-start.5 = (bf16[136,512]{1,0:T(8,128)(2,1)S(1)}, bf16[136,512]{1,0:T(8,128)(2,1)S(1)}, u32[]{:S(2)}, u32[]{:S(2)}) collective-permute-start(bf16[136,512]{1,0:T(8,128)(2,1)S(1)} %get-tuple-element.20), channel_id=1, source_target_pairs={{0,96},{1,97},{32,128},{33,129},{64,160},{65,161},{96,192},{97,193... | collective-permute-start | bytes 417800 | tf_op jit(solution)/shard_map/ppermute | solution.py:97
  20.5 9.1 %collective-permute-done.2.refs_3_ = bf16[136,512]{1,0:T(8,128)(2,1)S(1)} collective-permute-done((bf16[136,512]{1,0:T(8,128)(2,1)S(1)}, bf16[136,512]{1,0:T(8,128)(2,1)S(1)}, u32[]{:S(2)}, u32[]{:S(2)}) %collective-permute-start.2) | collective-permute-done | bytes 139296 | tf_op jit(solution)/shard_map/ppermute | solution.py:97
  29.6 0.0 collective-permute-done.3.refs_4_
  29.6 0.0 collective-permute-done.refs_1_
  29.7 1.9 %collective-permute-start.9 = (bf16[5,136,512]{2,1,0:T(8,128)(2,1)S(1)}, bf16[5,136,512]{2,1,0:T(8,128)(2,1)S(1)}, u32[]{:S(2)}, u32[]{:S(2)}) collective-permute-start(bf16[5,136,512]{2,1,0:T(8,128)(2,1)S(1)} %collect_kernel.2.refs_0_), channel_id=1, source_target_pairs={{1,2},{2,1},{3,4},{4,3},{5,6},{6,5},{7,8},{8,7},{9,10},{10,9},{11,... | collective-permute-start | bytes 2088968 | tf_op jit(solution)/shard_map/ppermute | solution.py:425
  31.6 0.1 collective-permute-start.7
  31.7 4.2 %collective-permute-start.6 = (bf16[136,512]{1,0:T(8,128)(2,1)S(1)}, bf16[136,512]{1,0:T(8,128)(2,1)S(1)}, u32[]{:S(2)}, u32[]{:S(2)}) collective-permute-start(bf16[136,512]{1,0:T(8,128)(2,1)S(1)} %slice_bitcast_fusion), channel_id=1, source_target_pairs={{0,64},{1,193},{32,96},{33,225},{64,128},{65,1},{96,160},{97,33},{... | collective-permute-start | bytes 417800 | tf_op jit(solution)/shard_map/ppermute | solution.py:97
  35.9 0.0 collective-permute-done.4.refs_0_
  35.9 0.0 collective-permute-done.5.refs_1_
  35.9 2.3 %collective-permute-done.6.refs_2_ = bf16[136,512]{1,0:T(8,128)(2,1)S(1)} collective-permute-done((bf16[136,512]{1,0:T(8,128)(2,1)S(1)}, bf16[136,512]{1,0:T(8,128)(2,1)S(1)}, u32[]{:S(2)}, u32[]{:S(2)}) %collective-permute-start.6) | collective-permute-done | bytes 139296 | tf_op jit(solution)/shard_map/ppermute | solution.py:97
  38.2 4.8 %collective-permute-start.10 = (bf16[3,136,512]{2,1,0:T(8,128)(2,1)S(1)}, bf16[3,136,512]{2,1,0:T(8,128)(2,1)S(1)}, u32[]{:S(2)}, u32[]{:S(2)}) collective-permute-start(bf16[3,136,512]{2,1,0:T(8,128)(2,1)S(1)} %collect_kernel.3.refs_1_), channel_id=1, source_target_pairs={{1,2},{2,1},{3,4},{4,3},{5,6},{6,5},{7,8},{8,7},{9,10},{10,9},{11,... | collective-permute-start | bytes 1253384 | tf_op jit(solution)/shard_map/ppermute | solution.py:425
  43.1 0.1 collective-permute-start.8
  43.2 5.6 %collective-permute-done.10.refs_5_ = bf16[3,136,512]{2,1,0:T(8,128)(2,1)S(1)} collective-permute-done((bf16[3,136,512]{2,1,0:T(8,128)(2,1)S(1)}, bf16[3,136,512]{2,1,0:T(8,128)(2,1)S(1)}, u32[]{:S(2)}, u32[]{:S(2)}) %collective-permute-start.10) | collective-permute-done | bytes 417824 | tf_op jit(solution)/shard_map/ppermute | solution.py:425
  48.8 0.0 collective-permute-done.8.refs_3_
  48.8 0.0 collective-permute-done.9.refs_4_
  48.8 0.0 collective-permute-done.7.refs_2_
  48.8 3.5 %gram_kernel.1 = (bf16[3,512,512]{2,1,0:T(8,128)(2,1)S(1)}, f32[5,128,128]{2,1,0:T(8,128)S(1)}, f32[5,128,128]{2,1,0:T(8,128)S(1)}) custom-call(s32[4]{0:T(128)S(1)} %pad_add_fusion.where_ref, bf16[5,136,512]{2,1,0:T(8,128)(2,1)S(1)} %collect_kernel.2.refs_0_, bf16[3,136,512]{2,1,0:T(8,128)(2,1)S(1)} %collect_kernel.3.refs_1_, ...), custom_call_target="tpu_custom_call" | custom-call | tf_op jit(solution)/shard_map/gram_kernel/pallas_call | solution.py:191
  52.3 0.1 collective-permute-start.11
  52.4 1.6 %collective-permute-done.11 = f32[5,128,128]{2,1,0:T(8,128)S(1)} collective-permute-done((f32[5,128,128]{2,1,0:T(8,128)S(1)}, f32[5,128,128]{2,1,0:T(8,128)S(1)}, u32[]{:S(2)}, u32[]{:S(2)}) %collective-permute-start.11) | collective-permute-done | bytes 327712 | tf_op jit(solution)/shard_map/ppermute | solution.py:402
  54.1 16.3 %all_to_all.15 = f32[16,40,128]{2,1,0:T(8,128)S(1)} all-to-all(f32[16,40,128]{2,1,0:T(8,128)S(1)} %bitcast.20), channel_id=1, replica_groups=mesh['z'=8,'x'=4,'y'=4,'core'=2] {'x','y'}, dimensions={0} | all-to-all | bytes 655360 | tf_op jit(solution)/shard_map/all_to_all | solution.py:405
  70.4 11.9 %all_to_all.16 = f32[8,40,128]{2,1,0:T(8,128)S(1)} all-to-all(f32[8,40,128]{2,1,0:T(8,128)S(1)} %broadcast_in_dim.6), channel_id=1, replica_groups=mesh['z'=8,'x'=4,'y'=4,'core'=2] {'z'}, dimensions={0} | all-to-all | bytes 327680 | tf_op jit(solution)/shard_map/all_to_all | solution.py:407
  82.4 11.5 %all_to_all.17 = f32[16,40,128]{2,1,0:T(8,128)S(1)} all-to-all(f32[16,40,128]{2,1,0:T(8,128)S(1)} %broadcast_in_dim.7), channel_id=1, replica_groups=mesh['z'=8,'x'=4,'y'=4,'core'=2] {'x','y'}, dimensions={0} | all-to-all | bytes 655360 | tf_op jit(solution)/shard_map/all_to_all | solution.py:409
  93.9 4.3 %collective-permute-start.12 = (f32[5,128,128]{2,1,0:T(8,128)S(1)}, f32[5,128,128]{2,1,0:T(8,128)S(1)}, u32[]{:S(2)}, u32[]{:S(2)}) collective-permute-start(f32[5,128,128]{2,1,0:T(8,128)S(1)} %bitcast.18), channel_id=1, source_target_pairs={{0,1},{1,0},{2,3},{3,2},{4,5},{5,4},{6,7},{7,6},{8,9},{9,8},{10,11... | collective-permute-start | bytes 983048 | tf_op jit(solution)/shard_map/ppermute | solution.py:410
  98.2 1.3 %collective-permute-done.12.other_ref = f32[5,128,128]{2,1,0:T(8,128)S(1)} collective-permute-done((f32[5,128,128]{2,1,0:T(8,128)S(1)}, f32[5,128,128]{2,1,0:T(8,128)S(1)}, u32[]{:S(2)}, u32[]{:S(2)}) %collective-permute-start.12) | collective-permute-done | bytes 327712 | tf_op jit(solution)/shard_map/ppermute | solution.py:410
  99.5 16.6 %factor_kernel.1 = (f32[512,512]{1,0:T(8,128)}, bf16[3,512,512]{2,1,0:T(8,128)(2,1)}) custom-call(s32[4]{0:T(128)S(1)} %pad_add_fusion.where_ref, f32[5,128,128]{2,1,0:T(8,128)S(1)} %bitcast.19, f32[5,128,128]{2,1,0:T(8,128)S(1)} %collective-permute-done.12.other_ref, bf16[3,512,512]{2,1,0:T(8,128)(2,1)S(1)} %get-tuple-element.23.snap_ref), custom_call_target="tpu_custom_call" | custom-call | tf_op jit(solution)/shard_map/factor_kernel/pallas_call | solution.py:380
  (8 shorter events, 0.2 us)
Async XLA Ops:
  3.5 26.2 %collective-permute-start = (bf16[2,136,512]{2,1,0:T(8,128)(2,1)S(1)}, bf16[2,136,512]{2,1,0:T(8,128)(2,1)S(1)}, u32[]{:S(2)}, u32[]{:S(2)}) collective-permute-start(bf16[2,136,512]{2,1,0:T(8,128)(2,1)S(1)} %get-tuple-element.15), channel_id=1, source_target_pairs={{0,64},{1,193},{32,96},{33,225},{64,128},{65,1},{96,160},{97,33},{... | collective-permute-start | bytes 835592 | tf_op jit(solution)/shard_map/ppermute | solution.py:97
  10.4 8.3 %collective-permute-start.1 = (bf16[136,512]{1,0:T(8,128)(2,1)S(1)}, bf16[136,512]{1,0:T(8,128)(2,1)S(1)}, u32[]{:S(2)}, u32[]{:S(2)}) collective-permute-start(bf16[136,512]{1,0:T(8,128)(2,1)S(1)} %get-tuple-element.16), channel_id=1, source_target_pairs={{0,192},{1,65},{32,224},{33,97},{64,0},{65,129},{96,32},{97,161},{... | collective-permute-start | bytes 417800 | tf_op jit(solution)/shard_map/ppermute | solution.py:97
  10.4 19.3 %collective-permute-start.2 = (bf16[136,512]{1,0:T(8,128)(2,1)S(1)}, bf16[136,512]{1,0:T(8,128)(2,1)S(1)}, u32[]{:S(2)}, u32[]{:S(2)}) collective-permute-start(bf16[136,512]{1,0:T(8,128)(2,1)S(1)} %get-tuple-element.17), channel_id=1, source_target_pairs={{0,224},{1,225},{32,0},{33,1},{64,32},{65,33},{96,64},{97,65},{128... | collective-permute-start | bytes 417800 | tf_op jit(solution)/shard_map/ppermute | solution.py:97
  13.5 16.1 %collective-permute-start.3 = (bf16[136,512]{1,0:T(8,128)(2,1)S(1)}, bf16[136,512]{1,0:T(8,128)(2,1)S(1)}, u32[]{:S(2)}, u32[]{:S(2)}) collective-permute-start(bf16[136,512]{1,0:T(8,128)(2,1)S(1)} %get-tuple-element.18), channel_id=1, source_target_pairs={{0,32},{1,33},{32,64},{33,65},{64,96},{65,97},{96,128},{97,129},{1... | collective-permute-start | bytes 417800 | tf_op jit(solution)/shard_map/ppermute | solution.py:97
  13.5 22.4 %collective-permute-start.4 = (bf16[136,512]{1,0:T(8,128)(2,1)S(1)}, bf16[136,512]{1,0:T(8,128)(2,1)S(1)}, u32[]{:S(2)}, u32[]{:S(2)}) collective-permute-start(bf16[136,512]{1,0:T(8,128)(2,1)S(1)} %get-tuple-element.19), channel_id=1, source_target_pairs={{0,160},{1,161},{32,192},{33,193},{64,224},{65,225},{96,0},{97,1},... | collective-permute-start | bytes 417800 | tf_op jit(solution)/shard_map/ppermute | solution.py:97
  18.7 17.3 %collective-permute-start.5 = (bf16[136,512]{1,0:T(8,128)(2,1)S(1)}, bf16[136,512]{1,0:T(8,128)(2,1)S(1)}, u32[]{:S(2)}, u32[]{:S(2)}) collective-permute-start(bf16[136,512]{1,0:T(8,128)(2,1)S(1)} %get-tuple-element.20), channel_id=1, source_target_pairs={{0,96},{1,97},{32,128},{33,129},{64,160},{65,161},{96,192},{97,193... | collective-permute-start | bytes 417800 | tf_op jit(solution)/shard_map/ppermute | solution.py:97
  29.7 19.1 %collective-permute-start.9 = (bf16[5,136,512]{2,1,0:T(8,128)(2,1)S(1)}, bf16[5,136,512]{2,1,0:T(8,128)(2,1)S(1)}, u32[]{:S(2)}, u32[]{:S(2)}) collective-permute-start(bf16[5,136,512]{2,1,0:T(8,128)(2,1)S(1)} %collect_kernel.2.refs_0_), channel_id=1, source_target_pairs={{1,2},{2,1},{3,4},{4,3},{5,6},{6,5},{7,8},{8,7},{9,10},{10,9},{11,... | collective-permute-start | bytes 2088968 | tf_op jit(solution)/shard_map/ppermute | solution.py:425
  31.6 17.2 %collective-permute-start.7 = (bf16[5,136,512]{2,1,0:T(8,128)(2,1)S(1)}, bf16[5,136,512]{2,1,0:T(8,128)(2,1)S(1)}, u32[]{:S(2)}, u32[]{:S(2)}) collective-permute-start(bf16[5,136,512]{2,1,0:T(8,128)(2,1)S(1)} %collect_kernel.2.refs_0_), channel_id=1, source_target_pairs={{0,1},{1,0},{2,3},{3,2},{4,5},{5,4},{6,7},{7,6},{8,9},{9,8},{10,11... | collective-permute-start | bytes 2088968 | tf_op jit(solution)/shard_map/ppermute | solution.py:424
  31.7 6.5 %collective-permute-start.6 = (bf16[136,512]{1,0:T(8,128)(2,1)S(1)}, bf16[136,512]{1,0:T(8,128)(2,1)S(1)}, u32[]{:S(2)}, u32[]{:S(2)}) collective-permute-start(bf16[136,512]{1,0:T(8,128)(2,1)S(1)} %slice_bitcast_fusion), channel_id=1, source_target_pairs={{0,64},{1,193},{32,96},{33,225},{64,128},{65,1},{96,160},{97,33},{... | collective-permute-start | bytes 417800 | tf_op jit(solution)/shard_map/ppermute | solution.py:97
  38.2 10.5 %collective-permute-start.10 = (bf16[3,136,512]{2,1,0:T(8,128)(2,1)S(1)}, bf16[3,136,512]{2,1,0:T(8,128)(2,1)S(1)}, u32[]{:S(2)}, u32[]{:S(2)}) collective-permute-start(bf16[3,136,512]{2,1,0:T(8,128)(2,1)S(1)} %collect_kernel.3.refs_1_), channel_id=1, source_target_pairs={{1,2},{2,1},{3,4},{4,3},{5,6},{6,5},{7,8},{8,7},{9,10},{10,9},{11,... | collective-permute-start | bytes 1253384 | tf_op jit(solution)/shard_map/ppermute | solution.py:425
  43.1 5.7 %collective-permute-start.8 = (bf16[3,136,512]{2,1,0:T(8,128)(2,1)S(1)}, bf16[3,136,512]{2,1,0:T(8,128)(2,1)S(1)}, u32[]{:S(2)}, u32[]{:S(2)}) collective-permute-start(bf16[3,136,512]{2,1,0:T(8,128)(2,1)S(1)} %collect_kernel.3.refs_1_), channel_id=1, source_target_pairs={{0,1},{1,0},{2,3},{3,2},{4,5},{5,4},{6,7},{7,6},{8,9},{9,8},{10,11... | collective-permute-start | bytes 1253384 | tf_op jit(solution)/shard_map/ppermute | solution.py:424
  52.3 1.7 %collective-permute-start.11 = (f32[5,128,128]{2,1,0:T(8,128)S(1)}, f32[5,128,128]{2,1,0:T(8,128)S(1)}, u32[]{:S(2)}, u32[]{:S(2)}) collective-permute-start(f32[5,128,128]{2,1,0:T(8,128)S(1)} %get-tuple-element.22), channel_id=1, source_target_pairs={{0,1},{1,0},{2,3},{3,2},{4,5},{5,4},{6,7},{7,6},{8,9},{9,8},{10,11... | collective-permute-start | bytes 983048 | tf_op jit(solution)/shard_map/ppermute | solution.py:402
  93.9 5.6 %collective-permute-start.12 = (f32[5,128,128]{2,1,0:T(8,128)S(1)}, f32[5,128,128]{2,1,0:T(8,128)S(1)}, u32[]{:S(2)}, u32[]{:S(2)}) collective-permute-start(f32[5,128,128]{2,1,0:T(8,128)S(1)} %bitcast.18), channel_id=1, source_target_pairs={{0,1},{1,0},{2,3},{3,2},{4,5},{5,4},{6,7},{7,6},{8,9},{9,8},{10,11... | collective-permute-start | bytes 983048 | tf_op jit(solution)/shard_map/ppermute | solution.py:410

commit v5 on v4

--- a/solution.py
+++ b/solution.py
@@ -243,7 +243,7 @@
                 a[i, j] = spread_ref[step % 2, pl.ds(j * SUB + i, SUB, stride=0), :]
         inside = (lane >= base) & (lane < base + SUB)
         seeded = jnp.where(inside, (lane - base == sub).astype(F32), block)
-        spread_ref[step % 2, SUB * SUB:, :] = seeded
+        spread_ref[step % 2, SUB * SUB:SUB * (SUB + 1), :] = seeded
         v = [spread_ref[step % 2, pl.ds(SUB * SUB + i, SUB, stride=0), :] for i in range(SUB)]
         unit = {}
         pivot, root = [], []
@@ -388,7 +388,7 @@
             pltpu.VMEM((blocks, 3, BLOCK, n), BF16),
             pltpu.VMEM((n, n), F32),
             pltpu.VMEM(snap.shape, BF16),
-            pltpu.VMEM((2, SUB * (SUB + 1), BLOCK), F32),
+            pltpu.VMEM((2, SUB * (SUB + 2), BLOCK), F32),
             pltpu.SemaphoreType.DMA((2, blocks)),
         ],
         compiler_params=PARAMS,

time: 116 us -> 116 us (level)
  no operation moved by 1% of the time
where the time goes in v5:
time: 116 us
  blocking collectives  39.7 us (34%)
  starting transfers between devices  29 us (25%)
  waiting for transfers between devices  23.4 us (20%)
  Pallas kernels  21.1 us (18%)
  local copies, waits for them, and re-layouts  1.85 us (2%)
    ppermute x7, starting transfers between devices, shifted(): return lax.ppermute(block, ('z', 'core'), pairs)  17.7 us
    pallas_call x1, Pallas kernels, factorize(): pl.pallas_call(functools.partial(factor_kernel, scale=scale), in_specs=[S...  16.5 us
    all_to_all x1, blocking collectives, sum_devices(): lax.all_to_all(kept.reshape(plane, part, width), ('x', 'y'), 0, 0, tiled=...  16.3 us
    ppermute x7, waiting for transfers between devices, shifted(): return lax.ppermute(block, ('z', 'core'), pairs)  15 us
    all_to_all x1, blocking collectives, sum_devices(): piece = lax.all_to_all(copies, 'z', 0, 0, tiled=True).sum(0)  11.9 us
    all_to_all x1, blocking collectives, sum_devices(): kept = lax.all_to_all(copies, ('x', 'y'), 0, 0, tiled=True).reshape(shape)  11.5 us
    ppermute x2, starting transfers between devices, local(): outer = [lax.ppermute(part, TILE, between) for part in (first, second)]  6.75 us
    ppermute x2, waiting for transfers between devices, local(): outer = [lax.ppermute(part, TILE, between) for part in (first, second)]  5.61 us
  transfers between devices with their start and end apart: 13, of which 6 were waited for; matrix products, arithmetic and copies ran while one was open for 0% of the time, Pallas kernels for 0%

profile of v5, /device:TPU:1, one launch (start us, length us, event | category | flops | bytes accessed | tf_op | source)
XLA Modules:
  0.0 116.2 jit_solution(1588601411384740280)
XLA Ops:
  0.6 1.8 %copy.8 = bf16[64,2,1,4096]{3,0,1,2:T(8,128)(2,1)S(1)} copy(bf16[64,2,1,4096]{3,1,2,0:T(2,128)(2,1)} %param.1) | data formatting | bytes 2097152 | tf_op args[0]
  2.5 0.1 pad_add_fusion.where_ref
  2.5 0.9 spread_kernel.1
  3.5 6.9 %collective-permute-start = (bf16[2,136,512]{2,1,0:T(8,128)(2,1)S(1)}, bf16[2,136,512]{2,1,0:T(8,128)(2,1)S(1)}, u32[]{:S(2)}, u32[]{:S(2)}) collective-permute-start(bf16[2,136,512]{2,1,0:T(8,128)(2,1)S(1)} %get-tuple-element.15), channel_id=1, source_target_pairs={{0,64},{1,193},{32,96},{33,225},{64,128},{65,1},{96,160},{97,33},{... | collective-permute-start | bytes 835592 | tf_op jit(solution)/shard_map/ppermute | solution.py:97
  10.4 0.0 collective-permute-start.1
  10.4 3.1 %collective-permute-start.2 = (bf16[136,512]{1,0:T(8,128)(2,1)S(1)}, bf16[136,512]{1,0:T(8,128)(2,1)S(1)}, u32[]{:S(2)}, u32[]{:S(2)}) collective-permute-start(bf16[136,512]{1,0:T(8,128)(2,1)S(1)} %get-tuple-element.17), channel_id=1, source_target_pairs={{0,224},{1,225},{32,0},{33,1},{64,32},{65,33},{96,64},{97,65},{128... | collective-permute-start | bytes 417800 | tf_op jit(solution)/shard_map/ppermute | solution.py:97
  13.5 0.0 collective-permute-start.3
  13.5 1.6 %collective-permute-start.4 = (bf16[136,512]{1,0:T(8,128)(2,1)S(1)}, bf16[136,512]{1,0:T(8,128)(2,1)S(1)}, u32[]{:S(2)}, u32[]{:S(2)}) collective-permute-start(bf16[136,512]{1,0:T(8,128)(2,1)S(1)} %get-tuple-element.19), channel_id=1, source_target_pairs={{0,160},{1,161},{32,192},{33,193},{64,224},{65,225},{96,0},{97,1},... | collective-permute-start | bytes 417800 | tf_op jit(solution)/shard_map/ppermute | solution.py:97
  15.1 3.6 %collective-permute-done.1.refs_2_ = bf16[136,512]{1,0:T(8,128)(2,1)S(1)} collective-permute-done((bf16[136,512]{1,0:T(8,128)(2,1)S(1)}, bf16[136,512]{1,0:T(8,128)(2,1)S(1)}, u32[]{:S(2)}, u32[]{:S(2)}) %collective-permute-start.1) | collective-permute-done | bytes 139296 | tf_op jit(solution)/shard_map/ppermute | solution.py:97
  18.7 1.9 %collective-permute-start.5 = (bf16[136,512]{1,0:T(8,128)(2,1)S(1)}, bf16[136,512]{1,0:T(8,128)(2,1)S(1)}, u32[]{:S(2)}, u32[]{:S(2)}) collective-permute-start(bf16[136,512]{1,0:T(8,128)(2,1)S(1)} %get-tuple-element.20), channel_id=1, source_target_pairs={{0,96},{1,97},{32,128},{33,129},{64,160},{65,161},{96,192},{97,193... | collective-permute-start | bytes 417800 | tf_op jit(solution)/shard_map/ppermute | solution.py:97
  20.5 9.1 %collective-permute-done.2.refs_3_ = bf16[136,512]{1,0:T(8,128)(2,1)S(1)} collective-permute-done((bf16[136,512]{1,0:T(8,128)(2,1)S(1)}, bf16[136,512]{1,0:T(8,128)(2,1)S(1)}, u32[]{:S(2)}, u32[]{:S(2)}) %collective-permute-start.2) | collective-permute-done | bytes 139296 | tf_op jit(solution)/shard_map/ppermute | solution.py:97
  29.6 0.0 collective-permute-done.3.refs_4_
  29.6 0.0 collective-permute-done.refs_1_
  29.7 1.9 %collective-permute-start.9 = (bf16[5,136,512]{2,1,0:T(8,128)(2,1)S(1)}, bf16[5,136,512]{2,1,0:T(8,128)(2,1)S(1)}, u32[]{:S(2)}, u32[]{:S(2)}) collective-permute-start(bf16[5,136,512]{2,1,0:T(8,128)(2,1)S(1)} %collect_kernel.2.refs_0_), channel_id=1, source_target_pairs={{1,2},{2,1},{3,4},{4,3},{5,6},{6,5},{7,8},{8,7},{9,10},{10,9},{11,... | collective-permute-start | bytes 2088968 | tf_op jit(solution)/shard_map/ppermute | solution.py:425
  31.6 0.1 collective-permute-start.7
  31.7 4.2 %collective-permute-start.6 = (bf16[136,512]{1,0:T(8,128)(2,1)S(1)}, bf16[136,512]{1,0:T(8,128)(2,1)S(1)}, u32[]{:S(2)}, u32[]{:S(2)}) collective-permute-start(bf16[136,512]{1,0:T(8,128)(2,1)S(1)} %slice_bitcast_fusion), channel_id=1, source_target_pairs={{0,64},{1,193},{32,96},{33,225},{64,128},{65,1},{96,160},{97,33},{... | collective-permute-start | bytes 417800 | tf_op jit(solution)/shard_map/ppermute | solution.py:97
  35.9 0.0 collective-permute-done.4.refs_0_
  35.9 0.0 collective-permute-done.5.refs_1_
  35.9 2.3 %collective-permute-done.6.refs_2_ = bf16[136,512]{1,0:T(8,128)(2,1)S(1)} collective-permute-done((bf16[136,512]{1,0:T(8,128)(2,1)S(1)}, bf16[136,512]{1,0:T(8,128)(2,1)S(1)}, u32[]{:S(2)}, u32[]{:S(2)}) %collective-permute-start.6) | collective-permute-done | bytes 139296 | tf_op jit(solution)/shard_map/ppermute | solution.py:97
  38.2 4.8 %collective-permute-start.10 = (bf16[3,136,512]{2,1,0:T(8,128)(2,1)S(1)}, bf16[3,136,512]{2,1,0:T(8,128)(2,1)S(1)}, u32[]{:S(2)}, u32[]{:S(2)}) collective-permute-start(bf16[3,136,512]{2,1,0:T(8,128)(2,1)S(1)} %collect_kernel.3.refs_1_), channel_id=1, source_target_pairs={{1,2},{2,1},{3,4},{4,3},{5,6},{6,5},{7,8},{8,7},{9,10},{10,9},{11,... | collective-permute-start | bytes 1253384 | tf_op jit(solution)/shard_map/ppermute | solution.py:425
  43.1 0.1 collective-permute-start.8
  43.2 5.6 %collective-permute-done.10.refs_5_ = bf16[3,136,512]{2,1,0:T(8,128)(2,1)S(1)} collective-permute-done((bf16[3,136,512]{2,1,0:T(8,128)(2,1)S(1)}, bf16[3,136,512]{2,1,0:T(8,128)(2,1)S(1)}, u32[]{:S(2)}, u32[]{:S(2)}) %collective-permute-start.10) | collective-permute-done | bytes 417824 | tf_op jit(solution)/shard_map/ppermute | solution.py:425
  48.8 0.0 collective-permute-done.8.refs_3_
  48.8 0.0 collective-permute-done.9.refs_4_
  48.8 0.0 collective-permute-done.7.refs_2_
  48.8 3.5 %gram_kernel.1 = (bf16[3,512,512]{2,1,0:T(8,128)(2,1)S(1)}, f32[5,128,128]{2,1,0:T(8,128)S(1)}, f32[5,128,128]{2,1,0:T(8,128)S(1)}) custom-call(s32[4]{0:T(128)S(1)} %pad_add_fusion.where_ref, bf16[5,136,512]{2,1,0:T(8,128)(2,1)S(1)} %collect_kernel.2.refs_0_, bf16[3,136,512]{2,1,0:T(8,128)(2,1)S(1)} %collect_kernel.3.refs_1_, ...), custom_call_target="tpu_custom_call" | custom-call | tf_op jit(solution)/shard_map/gram_kernel/pallas_call | solution.py:191
  52.3 0.1 collective-permute-start.11
  52.4 1.6 %collective-permute-done.11 = f32[5,128,128]{2,1,0:T(8,128)S(1)} collective-permute-done((f32[5,128,128]{2,1,0:T(8,128)S(1)}, f32[5,128,128]{2,1,0:T(8,128)S(1)}, u32[]{:S(2)}, u32[]{:S(2)}) %collective-permute-start.11) | collective-permute-done | bytes 327712 | tf_op jit(solution)/shard_map/ppermute | solution.py:402
  54.1 16.3 %all_to_all.15 = f32[16,40,128]{2,1,0:T(8,128)S(1)} all-to-all(f32[16,40,128]{2,1,0:T(8,128)S(1)} %bitcast.20), channel_id=1, replica_groups=mesh['z'=8,'x'=4,'y'=4,'core'=2] {'x','y'}, dimensions={0} | all-to-all | bytes 655360 | tf_op jit(solution)/shard_map/all_to_all | solution.py:405
  70.4 11.9 %all_to_all.16 = f32[8,40,128]{2,1,0:T(8,128)S(1)} all-to-all(f32[8,40,128]{2,1,0:T(8,128)S(1)} %broadcast_in_dim.6), channel_id=1, replica_groups=mesh['z'=8,'x'=4,'y'=4,'core'=2] {'z'}, dimensions={0} | all-to-all | bytes 327680 | tf_op jit(solution)/shard_map/all_to_all | solution.py:407
  82.4 11.5 %all_to_all.17 = f32[16,40,128]{2,1,0:T(8,128)S(1)} all-to-all(f32[16,40,128]{2,1,0:T(8,128)S(1)} %broadcast_in_dim.7), channel_id=1, replica_groups=mesh['z'=8,'x'=4,'y'=4,'core'=2] {'x','y'}, dimensions={0} | all-to-all | bytes 655360 | tf_op jit(solution)/shard_map/all_to_all | solution.py:409
  93.9 4.3 %collective-permute-start.12 = (f32[5,128,128]{2,1,0:T(8,128)S(1)}, f32[5,128,128]{2,1,0:T(8,128)S(1)}, u32[]{:S(2)}, u32[]{:S(2)}) collective-permute-start(f32[5,128,128]{2,1,0:T(8,128)S(1)} %bitcast.18), channel_id=1, source_target_pairs={{0,1},{1,0},{2,3},{3,2},{4,5},{5,4},{6,7},{7,6},{8,9},{9,8},{10,11... | collective-permute-start | bytes 983048 | tf_op jit(solution)/shard_map/ppermute | solution.py:410
  98.2 1.3 %collective-permute-done.12.other_ref = f32[5,128,128]{2,1,0:T(8,128)S(1)} collective-permute-done((f32[5,128,128]{2,1,0:T(8,128)S(1)}, f32[5,128,128]{2,1,0:T(8,128)S(1)}, u32[]{:S(2)}, u32[]{:S(2)}) %collective-permute-start.12) | collective-permute-done | bytes 327712 | tf_op jit(solution)/shard_map/ppermute | solution.py:410
  99.5 16.5 %factor_kernel.1 = (f32[512,512]{1,0:T(8,128)}, bf16[3,512,512]{2,1,0:T(8,128)(2,1)}) custom-call(s32[4]{0:T(128)S(1)} %pad_add_fusion.where_ref, f32[5,128,128]{2,1,0:T(8,128)S(1)} %bitcast.19, f32[5,128,128]{2,1,0:T(8,128)S(1)} %collective-permute-done.12.other_ref, bf16[3,512,512]{2,1,0:T(8,128)(2,1)S(1)} %get-tuple-element.23.snap_ref), custom_call_target="tpu_custom_call" | custom-call | tf_op jit(solution)/shard_map/factor_kernel/pallas_call | solution.py:380
  (8 shorter events, 0.2 us)
Async XLA Ops:
  3.5 26.2 %collective-permute-start = (bf16[2,136,512]{2,1,0:T(8,128)(2,1)S(1)}, bf16[2,136,512]{2,1,0:T(8,128)(2,1)S(1)}, u32[]{:S(2)}, u32[]{:S(2)}) collective-permute-start(bf16[2,136,512]{2,1,0:T(8,128)(2,1)S(1)} %get-tuple-element.15), channel_id=1, source_target_pairs={{0,64},{1,193},{32,96},{33,225},{64,128},{65,1},{96,160},{97,33},{... | collective-permute-start | bytes 835592 | tf_op jit(solution)/shard_map/ppermute | solution.py:97
  10.4 8.3 %collective-permute-start.1 = (bf16[136,512]{1,0:T(8,128)(2,1)S(1)}, bf16[136,512]{1,0:T(8,128)(2,1)S(1)}, u32[]{:S(2)}, u32[]{:S(2)}) collective-permute-start(bf16[136,512]{1,0:T(8,128)(2,1)S(1)} %get-tuple-element.16), channel_id=1, source_target_pairs={{0,192},{1,65},{32,224},{33,97},{64,0},{65,129},{96,32},{97,161},{... | collective-permute-start | bytes 417800 | tf_op jit(solution)/shard_map/ppermute | solution.py:97
  10.4 19.3 %collective-permute-start.2 = (bf16[136,512]{1,0:T(8,128)(2,1)S(1)}, bf16[136,512]{1,0:T(8,128)(2,1)S(1)}, u32[]{:S(2)}, u32[]{:S(2)}) collective-permute-start(bf16[136,512]{1,0:T(8,128)(2,1)S(1)} %get-tuple-element.17), channel_id=1, source_target_pairs={{0,224},{1,225},{32,0},{33,1},{64,32},{65,33},{96,64},{97,65},{128... | collective-permute-start | bytes 417800 | tf_op jit(solution)/shard_map/ppermute | solution.py:97
  13.5 16.1 %collective-permute-start.3 = (bf16[136,512]{1,0:T(8,128)(2,1)S(1)}, bf16[136,512]{1,0:T(8,128)(2,1)S(1)}, u32[]{:S(2)}, u32[]{:S(2)}) collective-permute-start(bf16[136,512]{1,0:T(8,128)(2,1)S(1)} %get-tuple-element.18), channel_id=1, source_target_pairs={{0,32},{1,33},{32,64},{33,65},{64,96},{65,97},{96,128},{97,129},{1... | collective-permute-start | bytes 417800 | tf_op jit(solution)/shard_map/ppermute | solution.py:97
  13.5 22.4 %collective-permute-start.4 = (bf16[136,512]{1,0:T(8,128)(2,1)S(1)}, bf16[136,512]{1,0:T(8,128)(2,1)S(1)}, u32[]{:S(2)}, u32[]{:S(2)}) collective-permute-start(bf16[136,512]{1,0:T(8,128)(2,1)S(1)} %get-tuple-element.19), channel_id=1, source_target_pairs={{0,160},{1,161},{32,192},{33,193},{64,224},{65,225},{96,0},{97,1},... | collective-permute-start | bytes 417800 | tf_op jit(solution)/shard_map/ppermute | solution.py:97
  18.7 17.3 %collective-permute-start.5 = (bf16[136,512]{1,0:T(8,128)(2,1)S(1)}, bf16[136,512]{1,0:T(8,128)(2,1)S(1)}, u32[]{:S(2)}, u32[]{:S(2)}) collective-permute-start(bf16[136,512]{1,0:T(8,128)(2,1)S(1)} %get-tuple-element.20), channel_id=1, source_target_pairs={{0,96},{1,97},{32,128},{33,129},{64,160},{65,161},{96,192},{97,193... | collective-permute-start | bytes 417800 | tf_op jit(solution)/shard_map/ppermute | solution.py:97
  29.7 19.1 %collective-permute-start.9 = (bf16[5,136,512]{2,1,0:T(8,128)(2,1)S(1)}, bf16[5,136,512]{2,1,0:T(8,128)(2,1)S(1)}, u32[]{:S(2)}, u32[]{:S(2)}) collective-permute-start(bf16[5,136,512]{2,1,0:T(8,128)(2,1)S(1)} %collect_kernel.2.refs_0_), channel_id=1, source_target_pairs={{1,2},{2,1},{3,4},{4,3},{5,6},{6,5},{7,8},{8,7},{9,10},{10,9},{11,... | collective-permute-start | bytes 2088968 | tf_op jit(solution)/shard_map/ppermute | solution.py:425
  31.6 17.2 %collective-permute-start.7 = (bf16[5,136,512]{2,1,0:T(8,128)(2,1)S(1)}, bf16[5,136,512]{2,1,0:T(8,128)(2,1)S(1)}, u32[]{:S(2)}, u32[]{:S(2)}) collective-permute-start(bf16[5,136,512]{2,1,0:T(8,128)(2,1)S(1)} %collect_kernel.2.refs_0_), channel_id=1, source_target_pairs={{0,1},{1,0},{2,3},{3,2},{4,5},{5,4},{6,7},{7,6},{8,9},{9,8},{10,11... | collective-permute-start | bytes 2088968 | tf_op jit(solution)/shard_map/ppermute | solution.py:424
  31.7 6.5 %collective-permute-start.6 = (bf16[136,512]{1,0:T(8,128)(2,1)S(1)}, bf16[136,512]{1,0:T(8,128)(2,1)S(1)}, u32[]{:S(2)}, u32[]{:S(2)}) collective-permute-start(bf16[136,512]{1,0:T(8,128)(2,1)S(1)} %slice_bitcast_fusion), channel_id=1, source_target_pairs={{0,64},{1,193},{32,96},{33,225},{64,128},{65,1},{96,160},{97,33},{... | collective-permute-start | bytes 417800 | tf_op jit(solution)/shard_map/ppermute | solution.py:97
  38.2 10.5 %collective-permute-start.10 = (bf16[3,136,512]{2,1,0:T(8,128)(2,1)S(1)}, bf16[3,136,512]{2,1,0:T(8,128)(2,1)S(1)}, u32[]{:S(2)}, u32[]{:S(2)}) collective-permute-start(bf16[3,136,512]{2,1,0:T(8,128)(2,1)S(1)} %collect_kernel.3.refs_1_), channel_id=1, source_target_pairs={{1,2},{2,1},{3,4},{4,3},{5,6},{6,5},{7,8},{8,7},{9,10},{10,9},{11,... | collective-permute-start | bytes 1253384 | tf_op jit(solution)/shard_map/ppermute | solution.py:425
  43.1 5.7 %collective-permute-start.8 = (bf16[3,136,512]{2,1,0:T(8,128)(2,1)S(1)}, bf16[3,136,512]{2,1,0:T(8,128)(2,1)S(1)}, u32[]{:S(2)}, u32[]{:S(2)}) collective-permute-start(bf16[3,136,512]{2,1,0:T(8,128)(2,1)S(1)} %collect_kernel.3.refs_1_), channel_id=1, source_target_pairs={{0,1},{1,0},{2,3},{3,2},{4,5},{5,4},{6,7},{7,6},{8,9},{9,8},{10,11... | collective-permute-start | bytes 1253384 | tf_op jit(solution)/shard_map/ppermute | solution.py:424
  52.3 1.7 %collective-permute-start.11 = (f32[5,128,128]{2,1,0:T(8,128)S(1)}, f32[5,128,128]{2,1,0:T(8,128)S(1)}, u32[]{:S(2)}, u32[]{:S(2)}) collective-permute-start(f32[5,128,128]{2,1,0:T(8,128)S(1)} %get-tuple-element.22), channel_id=1, source_target_pairs={{0,1},{1,0},{2,3},{3,2},{4,5},{5,4},{6,7},{7,6},{8,9},{9,8},{10,11... | collective-permute-start | bytes 983048 | tf_op jit(solution)/shard_map/ppermute | solution.py:402
  93.9 5.6 %collective-permute-start.12 = (f32[5,128,128]{2,1,0:T(8,128)S(1)}, f32[5,128,128]{2,1,0:T(8,128)S(1)}, u32[]{:S(2)}, u32[]{:S(2)}) collective-permute-start(f32[5,128,128]{2,1,0:T(8,128)S(1)} %bitcast.18), channel_id=1, source_target_pairs={{0,1},{1,0},{2,3},{3,2},{4,5},{5,4},{6,7},{7,6},{8,9},{9,8},{10,11... | collective-permute-start | bytes 983048 | tf_op jit(solution)/shard_map/ppermute | solution.py:410
